TPU v7x, 32 devices: a whole 2x2x4 slice. The times are simulated.
32 devices in a mesh: dp: 8 (over y, x, core), ctx: 4 (over z).
Axes of the slice: x: 2, y: 2, z: 4, core: 2. Of those that a mesh axis runs over, the one named last changes fastest.
Arguments:
- frames: bfloat16 [8192, 1024], P(('dp', 'ctx')), parts along dimension 0, may hold values from -20 to 20
- tile_source: int32 [512], P('dp'), parts along dimension 0, may hold values from 0 to 63, as said below
- tile_utt: int32 [512], P('dp'), parts along dimension 0, may hold values from 0 to 3, never falling along the last dimension, each value on 1 to 33 neighbouring positions
- query_weight: bfloat16 [1024, 512], replicated, may hold values from -1.625 to 1.625
- key_weight: bfloat16 [1024, 512], replicated, may hold values from -0.1875 to 0.1875
- value_weight: bfloat16 [1024, 512], replicated, may hold values from -0.1875 to 0.1875
- output_weight: bfloat16 [512, 1024], replicated, may hold values from -1.5 to 1.5
- depth_weight: float32 [31, 1024], replicated, may hold values from -1 to 1
- bn_scale: float32 [1024], replicated, may hold values from 0.5 to 2
- bn_shift: float32 [1024], replicated, may hold values from -3 to 3
Outputs:
- encoded: bfloat16 [8192, 1024], P(('dp', 'ctx')), parts along dimension 0
There are 8 independent parts, one for each index of `dp`. A program takes and returns all parts, laid end to end along the dimension named above; an argument that names none is the same for every part. Nothing has to cross between parts.
Inputs may be any that keep to these rules, and one draw needn't show every extreme that they name: `tile_source`: A permutation of the tiles of a part. The tiles that one shard receives come at most 4 from any one shard, and exactly 4 from some shard; for one tile position within a shard, the sources over all shards lie on distinct shards. `tile_utt`: never falls along the tiles; each of the 4 utterances holds 1 to 33 tiles, one exactly 33.
All inputs are finite; a program needn't handle non-finite values.
Results may differ from a plain program's by a relative error of at most 0.0068.
Values may be sent and summed in bfloat16 or wider, within the bound.
No kernel may reach another device: no remote copies, remote signals or barrier semaphores. Data moves between devices by JAX's collectives and lax.ppermute only.
A program may use at most 64 MiB of HBM per device.

v0:
```python
import math

import jax
import jax.numpy as jnp
from jax import lax
from jax.sharding import PartitionSpec as P

HEADS = 4
HEAD_DIM = 128
KERNEL = 31
TILE = 16


NEGATIVE = -1e30


def extended_2(block, sides, width):
    for axis, dim in sides:
        count = lax.axis_size(axis)
        forward = [(i, i + 1) for i in range(count - 1)]
        backward = [(target, source) for source, target in forward]
        low = lax.ppermute(
            lax.slice_in_dim(block, block.shape[dim] - width, None, axis=dim), axis, forward
        )
        high = lax.ppermute(lax.slice_in_dim(block, 0, width, axis=dim), axis, backward)
        block = jnp.concatenate([low, block, high], axis=dim)
    return block


def layer_norm(rows):
    values = rows.astype(jnp.float32)
    center = values - jnp.mean(values, axis=-1, keepdims=True)
    spread = jnp.mean(center * center, axis=-1, keepdims=True)
    return center * lax.rsqrt(spread + 1e-05)


def local_utt(row_utt, first_row, rows_here, total_rows):
    positions = first_row + jnp.arange(rows_here, dtype=jnp.int32)
    inside = (positions >= 0) & (positions < total_rows)
    picked = jnp.take(row_utt, jnp.clip(positions, 0, total_rows - 1), axis=0)
    return jnp.where(inside, picked, -1)


def attend(carried, key_block, value_block, key_utt, queries, query_utt, score_scale):
    weighted, running_max, running_sum = carried
    scores = (
        jnp.einsum("qhd,khd->hqk", queries, key_block, preferred_element_type=jnp.float32)
        * score_scale
    )
    allowed = (query_utt[:, None] == key_utt[None, :])[None]
    block_max = jnp.max(jnp.where(allowed, scores, NEGATIVE), axis=-1, keepdims=True)
    new_max = jnp.maximum(running_max, block_max)
    factor = jnp.exp(running_max - new_max)
    weights = jnp.where(allowed, jnp.exp(scores - new_max), 0.0)
    running_sum = running_sum * factor + jnp.sum(weights, axis=-1, keepdims=True)
    weighted = weighted * factor + jnp.einsum(
        "hqk,khd->hqd",
        weights.astype(jnp.bfloat16),
        value_block,
        preferred_element_type=jnp.float32,
    )
    return (weighted, new_max, running_sum)


def pick_block(rows_here, rows_dev):
    shard_count = rows_here // rows_dev
    group_limit = max(1, 1024 // rows_dev)
    return rows_dev * max(
        [
            grouping
            for grouping in range(1, shard_count + 1)
            if shard_count % grouping == 0 and grouping <= group_limit
        ]
    )


def per_device(
    frames,
    tile_source,
    tile_utt,
    query_weight,
    key_weight,
    value_weight,
    output_weight,
    depth_weight,
    bn_scale,
    bn_shift,
):
    shard_count = lax.axis_size("ctx")
    my_index = lax.axis_index("ctx")
    rows_dev, feature_width = frames.shape
    tiles_dev = rows_dev // TILE
    tile_total = tiles_dev * shard_count
    total_rows = tile_total * TILE
    slot_count = (tiles_dev + shard_count - 1) // shard_count
    positions = jnp.arange(tile_total, dtype=jnp.int32)
    source_dev = tile_source // tiles_dev
    source_slot = tile_source % tiles_dev
    dest_dev = positions // tiles_dev
    earlier = (
        (dest_dev[:, None] == dest_dev[None, :])
        & (source_dev[:, None] == source_dev[None, :])
        & (positions[None, :] < positions[:, None])
    )
    arrival_rank = jnp.sum(earlier.astype(jnp.int32), axis=1)
    shards = jnp.arange(shard_count, dtype=jnp.int32)
    places = jnp.arange(slot_count, dtype=jnp.int32)
    matches = (
        (source_dev[None, None, :] == my_index)
        & (dest_dev[None, None, :] == shards[:, None, None])
        & (arrival_rank[None, None, :] == places[None, :, None])
    )
    chosen = jnp.sum(jnp.where(matches, source_slot[None, None, :], 0), axis=2).reshape(-1)
    filled = jnp.any(matches, axis=2).reshape(-1)
    tile_rows = frames.reshape(tiles_dev, TILE, feature_width)
    outgoing = jnp.where(
        filled[:, None, None], jnp.take(tile_rows, chosen, axis=0), jnp.zeros((), frames.dtype)
    )
    outgoing = outgoing.reshape(shard_count, slot_count, TILE, feature_width)
    arrived = lax.all_to_all(outgoing, "ctx", split_axis=0, concat_axis=0, tiled=True)
    mine_source = lax.dynamic_slice_in_dim(source_dev, my_index * tiles_dev, tiles_dev)
    mine_rank = lax.dynamic_slice_in_dim(arrival_rank, my_index * tiles_dev, tiles_dev)
    grouped = jnp.take(
        arrived.reshape(shard_count * slot_count, TILE, feature_width),
        mine_source * slot_count + mine_rank,
        axis=0,
    ).reshape(rows_dev, feature_width)
    normed = layer_norm(grouped).astype(jnp.bfloat16)
    queries = (
        jnp.dot(normed, query_weight, preferred_element_type=jnp.float32)
        .astype(jnp.bfloat16)
        .reshape(rows_dev, HEADS, HEAD_DIM)
    )
    key_rows = jnp.dot(normed, key_weight, preferred_element_type=jnp.float32).astype(jnp.bfloat16)
    value_rows = jnp.dot(normed, value_weight, preferred_element_type=jnp.float32).astype(
        jnp.bfloat16
    )
    key_value = jnp.stack([key_rows, value_rows])
    row_utt = jnp.repeat(tile_utt, TILE)
    query_utt = lax.dynamic_slice_in_dim(row_utt, my_index * rows_dev, rows_dev)
    score_scale = 1.0 / math.sqrt(HEAD_DIM)
    start_state = (
        jnp.zeros((HEADS, rows_dev, HEAD_DIM), jnp.float32),
        jnp.full((HEADS, rows_dev, 1), NEGATIVE, jnp.float32),
        jnp.zeros((HEADS, rows_dev, 1), jnp.float32),
    )

    def block_update(carried, block_pair, key_utt):
        rows_here = block_pair.shape[1]
        key_block = block_pair[0].reshape(rows_here, HEADS, HEAD_DIM)
        value_block = block_pair[1].reshape(rows_here, HEADS, HEAD_DIM)
        return attend(carried, key_block, value_block, key_utt, queries, query_utt, score_scale)

    fetched = lax.all_gather(key_value, "ctx", axis=1, tiled=True)
    rows_here = fetched.shape[1]
    block_rows = pick_block(rows_here, rows_dev)

    def one_block(block_index, inner):
        section = lax.dynamic_slice_in_dim(fetched, block_index * block_rows, block_rows, 1)
        key_utt = local_utt(row_utt, block_index * block_rows, block_rows, total_rows)
        return block_update(inner, section, key_utt)

    carried = lax.fori_loop(0, rows_here // block_rows, one_block, start_state)
    weighted, running_max, running_sum = carried
    attended = (
        jnp.transpose(weighted / running_sum, (1, 0, 2))
        .reshape(rows_dev, HEADS * HEAD_DIM)
        .astype(jnp.bfloat16)
    )
    residual = (
        grouped.astype(jnp.float32)
        + jnp.dot(attended, output_weight, preferred_element_type=jnp.float32)
    ).astype(jnp.bfloat16)
    shaped = layer_norm(residual).astype(jnp.bfloat16)
    margin = (KERNEL - 1) // 2
    extended = extended_2(shaped, (("ctx", 0),), margin).astype(jnp.float32)
    extended_utt = local_utt(
        row_utt, my_index * rows_dev - margin, rows_dev + 2 * margin, total_rows
    )
    convolved = jnp.zeros((rows_dev, feature_width), jnp.float32)
    for offset in range(KERNEL):
        aligned = (extended_utt[offset : offset + rows_dev] == query_utt)[:, None]
        convolved = (
            convolved
            + jnp.where(aligned, extended[offset : offset + rows_dev], 0.0) * depth_weight[offset]
        )
    activation = convolved * bn_scale + bn_shift
    return (residual.astype(jnp.float32) + activation * jax.nn.sigmoid(activation)).astype(
        jnp.bfloat16
    )


def solution(mesh):
    return jax.shard_map(
        per_device,
        mesh=mesh,
        in_specs=(P(("dp", "ctx"), None), P("dp"), P("dp"), P(), P(), P(), P(), P(), P(), P()),
        out_specs=P(("dp", "ctx"), None),
        check_vma=False,
    )
```

profile of v0, /device:TPU:0, one launch (start us, length us, event | category | flops | bytes accessed | tf_op | source)
XLA Modules:
  0.0 121.9 jit_solution(12822432287140586318)
XLA Ops:
  6.5 0.8 and_select_fusion.1
  7.4 0.7 broadcast_compare_fusion.1
  8.7 1.6 %gather_fusion.2 = bf16[16,16,1024]{2,1,0:T(8,128)(2,1)S(1)} fusion(bf16[16,16,1024]{2,1,0:T(8,128)(2,1)} %bitcast.80, s32[1024]{0:T(1024)S(1)} %pad_clamp_fusion.2), kind=kCustom, calls=%fused_computation.clone | custom fusion | bytes 1048640 | tf_op jit(solution)/shard_map/jit(_take)/gather | solution.py:117
  10.4 0.9 select_select_fusion
  11.3 6.3 %all-to-all-start = ((bf16[4,4,16,1024]{3,2,1,0:T(8,128)(2,1)}), bf16[4,4,16,1024]{3,2,1,0:T(8,128)(2,1)S(1)}, u32[]{:S(2)}, u32[]{:S(2)}) async-start(bf16[4,4,16,1024]{3,2,1,0:T(8,128)(2,1)} %bitcast.1), calls=%async_computation | async-start | bytes 1048576 | tf_op jit(solution)/shard_map/all_to_all | solution.py:120
  17.7 14.4 %all-to-all-done = bf16[4,4,16,1024]{3,2,1,0:T(8,128)(2,1)S(1)} async-done(((bf16[4,4,16,1024]{3,2,1,0:T(8,128)(2,1)}), bf16[4,4,16,1024]{3,2,1,0:T(8,128)(2,1)S(1)}, u32[]{:S(2)}, u32[]{:S(2)}) %all-to-all-start) | async-done | bytes 524320 | tf_op jit(solution)/shard_map/all_to_all | solution.py:120
  34.2 1.7 %fusion.19 = bf16[1,256,512]{2,1,0:T(8,128)(2,1)S(1)} fusion(bf16[256,1024]{1,0:T(8,128)(2,1)S(1)} %fusion.87, bf16[1024,512]{1,0:T(8,128)(2,1)} %param.17), kind=kOutput, calls=%fused_computation.27 | convolution fusion | flops 268566528 | bytes 1835008 | tf_op jit(solution)/shard_map/dot_general | solution.py:135
  35.9 0.8 pad_maximum_fusion
  36.9 1.7 %gather_fusion.1 = s32[286]{0:T(512)S(1)} fusion(s32[1024]{0:T(1024)S(1)} %reshape.320, s32[1024]{0:T(1024)S(1)} %pad_clamp_fusion), kind=kCustom, calls=%fused_computation.3 | custom fusion | bytes 3432 | tf_op jit(solution)/shard_map/jit(_take)/gather | solution.py:40
  38.6 4.5 %gather_fusion = s32[1024]{0:T(1024)S(1)} fusion(s32[1024]{0:T(1024)S(1)} %reshape.320, s32[1024]{0:T(1024)S(1)} %broadcast_clamp_fusion), kind=kCustom, calls=%fused_computation.2 | custom fusion | bytes 12288 | tf_op jit(solution)/shard_map/while/body/eval_jaxpr/jit(_take)/gather | solution.py:40
  43.8 0.7 slice_compare_fusion.29
  44.9 1.2 fusion.17
  46.2 35.4 %all-gather.2.cloned.1.call-done = bf16[2,1024,512]{2,1,0:T(8,128)(2,1)} async-done(((bf16[2,256,512]{2,1,0:T(8,128)(2,1)}), bf16[2,1024,512]{2,1,0:T(8,128)(2,1)}) %all-gather.2.cloned.1.call-update) | async-done | bytes 2097168 | tf_op jit(solution)/shard_map/all_gather | solution.py:154
  81.7 3.0 %fusion.111 = (bf16[1,1024,512]{2,1,0:T(8,128)(2,1)}, bf16[1,1024,512]{2,1,0:T(8,128)(2,1)}) fusion(bf16[2,1024,512]{2,1,0:T(8,128)(2,1)} %all-gather.2.cloned.1.call-done), kind=kLoop, calls=%fused_computation.224 | loop fusion | bytes 4194304 | tf_op jit(solution)/shard_map/while/body/eval_jaxpr/slice | solution.py:150
  84.7 2.2 %squeeze.8 = bf16[1024,4,128]{2,1,0:T(4,128)(2,1)} reshape(bf16[1,1024,512]{2,1,0:T(8,128)(2,1)} %get-tuple-element.38) | data formatting | bytes 2097152 | tf_op jit(solution)/shard_map/while/body/eval_jaxpr/reshape;while/body/eval_jaxpr/squeeze | solution.py:150
  86.8 2.3 %select_reduce_fusion = (f32[4,256]{1,0:T(4,128)S(1)}, f32[4,256,1024]{2,1,0:T(8,128)S(1)}) fusion(pred[256,1024]{1,0:T(8,128)(4,1)S(1)} %broadcast_compare_fusion, bf16[1024,4,128]{2,1,0:T(4,128)(2,1)} %squeeze.8, bf16[32,4,8,128]{3,2,1,0:T(8,128)(2,1)S(1)} %copy-done.4), kind=kOutput, calls=%fused_computation.5 | convolution fusion | flops 271580160 | bytes 5771264 | tf_op jit(solution)/shard_map/while/body/eval_jaxpr/qhd,khd->hqk/dot_general | solution.py:47
  89.2 1.9 %copy-done.1 = f32[4,256,1024]{2,1,0:T(8,128)} copy-done((f32[4,256,1024]{2,1,0:T(8,128)}, f32[4,256,1024]{2,1,0:T(8,128)S(1)}, u32[]{:S(2)}) %copy-start.1) | copy-done | bytes 4194328
  91.1 1.4 %fusion = f32[4,256]{1,0:T(4,128)S(1)} fusion(f32[4,256,1024]{2,1,0:T(8,128)S(1)} %get-tuple-element.107, f32[4,256]{1,0:T(4,128)S(1)} %get-tuple-element.75, pred[256,1024]{1,0:T(8,128)(4,1)S(1)} %broadcast_compare_fusion), kind=kLoop, calls=%fused_computation.6 | loop fusion | flops 4193280 | bytes 4464640 | tf_op jit(solution)/shard_map/while/body/eval_jaxpr/reduce_sum | solution.py:55
  92.5 2.3 %copy.20 = bf16[1,1024,512]{1,2,0:T(8,128)(2,1)} copy(bf16[1,1024,512]{2,1,0:T(8,128)(2,1)} %get-tuple-element.40) | data formatting | bytes 2097152 | tf_op jit(solution)/shard_map/while/body/eval_jaxpr/reshape;while/body/eval_jaxpr/squeeze | solution.py:151
  94.8 3.6 %fusion.93 = bf16[256,4,128]{0,2,1:T(8,128)(2,1)S(1)} fusion(bf16[1024,4,128]{0,2,1:T(8,128)(2,1)} %bitcast.79, f32[4,256,1024]{2,1,0:T(8,128)} %copy-done.1, f32[4,256]{1,0:T(4,128)S(1)} %get-tuple-element.75, pred[256,1024]{1,0:T(8,128)(4,1)S(1)} %broadcast_compare_fusion, f32[256,4]{0,1:T(4,128)S(1)} %bitcast_add_fusion, f32[256,4]{0,1:T(4,128)S(1)} %get-tuple-element.74), kind=kOutput, calls=%fused_computation.132 | convolution fusion | flops 273022976 | bytes 5779456 | tf_op jit(solution)/shard_map/while/body/eval_jaxpr/hqk,khd->hqd/dot_general | solution.py:56
  99.8 2.1 %collective-permute-start = (bf16[15,1024]{1,0:T(8,128)(2,1)S(1)}, bf16[15,1024]{1,0:T(8,128)(2,1)S(1)}, u32[]{:S(2)}, u32[]{:S(2)}) collective-permute-start(bf16[15,1024]{1,0:T(8,128)(2,1)S(1)} %get-tuple-element.41), channel_id=1, source_target_pairs={{0,1},{1,2},{2,3},{4,5},{5,6},{6,7},{8,9},{9,10},{10,11},{12,13},{... | collective-permute-start | bytes 92168 | tf_op jit(solution)/shard_map/ppermute | solution.py:22
  101.9 1.3 %collective-permute-start.1 = (bf16[15,1024]{1,0:T(8,128)(2,1)S(1)}, bf16[15,1024]{1,0:T(8,128)(2,1)S(1)}, u32[]{:S(2)}, u32[]{:S(2)}) collective-permute-start(bf16[15,1024]{1,0:T(8,128)(2,1)S(1)} %get-tuple-element.42), channel_id=1, source_target_pairs={{1,0},{2,1},{3,2},{5,4},{6,5},{7,6},{9,8},{10,9},{11,10},{13,12},{... | collective-permute-start | bytes 92168 | tf_op jit(solution)/shard_map/ppermute | solution.py:25
  103.4 4.2 %collective-permute-done.1 = bf16[15,1024]{1,0:T(8,128)(2,1)S(1)} collective-permute-done((bf16[15,1024]{1,0:T(8,128)(2,1)S(1)}, bf16[15,1024]{1,0:T(8,128)(2,1)S(1)}, u32[]{:S(2)}, u32[]{:S(2)}) %collective-permute-start.1) | collective-permute-done | bytes 30752 | tf_op jit(solution)/shard_map/ppermute | solution.py:25
  108.0 7.0 %fusion.22 = bf16[256,1024]{1,0:T(8,128)(2,1)} fusion(bf16[256,1024]{1,0:T(8,128)(2,1)S(1)} %get-tuple-element.109, f32[286,1024]{1,0:T(8,128)S(1)} %maximum_convert_fusion, f32[1024]{0:T(1024)S(1)} %copy-done.6, f32[1024]{0:T(1024)S(1)} %copy-done.7, f32[1024]{0:T(1024)S(1)} %bitcast.92, f32[1024]{0:T(1024)S(1)} %bitcast.93, f32[1024]{0:T(1024)S(1)} %bitcast.95, ...), kind=kLoop, calls=%fused_computation.30 | loop fusion | flops 26476544 | bytes 33697536 | tf_op jit(solution)/shard_map/convert_element_type | solution.py:188
  (100 shorter events, 5.7 us)
Async XLA Ops:
  6.5 92.1 %copy-start = (bf16[512,1024]{1,0:T(8,128)(2,1)S(1)}, bf16[512,1024]{1,0:T(8,128)(2,1)}, u32[]{:S(2)}) copy-start(bf16[512,1024]{1,0:T(8,128)(2,1)} %param.18) | copy-start | bytes 3145732
  6.5 27.2 %copy-start.2 = (bf16[1024,512]{1,0:T(8,128)(2,1)S(1)}, bf16[1024,512]{1,0:T(8,128)(2,1)}, u32[]{:S(2)}) copy-start(bf16[1024,512]{1,0:T(8,128)(2,1)} %param.16) | copy-start | bytes 3145732
  11.3 20.8 %all-to-all-start = ((bf16[4,4,16,1024]{3,2,1,0:T(8,128)(2,1)}), bf16[4,4,16,1024]{3,2,1,0:T(8,128)(2,1)S(1)}, u32[]{:S(2)}, u32[]{:S(2)}) async-start(bf16[4,4,16,1024]{3,2,1,0:T(8,128)(2,1)} %bitcast.1), calls=%async_computation | async-start | bytes 1048576 | tf_op jit(solution)/shard_map/all_to_all | solution.py:120
  17.6 64.0 %all-gather.2.cloned.1.call-start = ((), (), s32[]{:S(2)}) async-start(), calls=%async_computation.1 | async-start | bytes 2621440 | tf_op jit(solution)/shard_map/all_gather | solution.py:154
  46.1 40.8 %copy-start.4 = (bf16[32,4,8,128]{3,2,1,0:T(8,128)(2,1)S(1)}, bf16[32,4,8,128]{3,2,1,0:T(8,128)(2,1)}, u32[]{:S(2)}) copy-start(bf16[32,4,8,128]{3,2,1,0:T(8,128)(2,1)} %fusion.17) | copy-start | bytes 786436
  98.4 9.4 %copy-start.6 = (f32[1024]{0:T(1024)S(1)}, f32[1024]{0:T(1024)}, u32[]{:S(2)}) copy-start(f32[1024]{0:T(1024)} %param.21) | copy-start | bytes 12292
  98.4 9.4 %copy-start.7 = (f32[1024]{0:T(1024)S(1)}, f32[1024]{0:T(1024)}, u32[]{:S(2)}) copy-start(f32[1024]{0:T(1024)} %param.20) | copy-start | bytes 12292
  98.4 9.4 %copy-start.8 = (pred[256]{0:T(512)(128)(4,1)S(1)}, pred[256]{0:T(512)(128)(4,1)}, u32[]{:S(2)}) copy-start(pred[256]{0:T(512)(128)(4,1)} %get-tuple-element.77) | copy-start | bytes 772
  98.4 9.4 %copy-start.9 = (pred[256]{0:T(512)(128)(4,1)S(1)}, pred[256]{0:T(512)(128)(4,1)}, u32[]{:S(2)}) copy-start(pred[256]{0:T(512)(128)(4,1)} %get-tuple-element.78) | copy-start | bytes 772
  98.4 9.4 %copy-start.10 = (pred[256]{0:T(512)(128)(4,1)S(1)}, pred[256]{0:T(512)(128)(4,1)}, u32[]{:S(2)}) copy-start(pred[256]{0:T(512)(128)(4,1)} %get-tuple-element.79) | copy-start | bytes 772
  98.5 9.4 %copy-start.11 = (pred[256]{0:T(512)(128)(4,1)S(1)}, pred[256]{0:T(512)(128)(4,1)}, u32[]{:S(2)}) copy-start(pred[256]{0:T(512)(128)(4,1)} %get-tuple-element.80) | copy-start | bytes 772
  98.5 9.4 %copy-start.12 = (pred[256]{0:T(512)(128)(4,1)S(1)}, pred[256]{0:T(512)(128)(4,1)}, u32[]{:S(2)}) copy-start(pred[256]{0:T(512)(128)(4,1)} %get-tuple-element.81) | copy-start | bytes 772
  98.5 9.4 %copy-start.13 = (pred[256]{0:T(512)(128)(4,1)S(1)}, pred[256]{0:T(512)(128)(4,1)}, u32[]{:S(2)}) copy-start(pred[256]{0:T(512)(128)(4,1)} %get-tuple-element.82) | copy-start | bytes 772
  98.5 9.4 %copy-start.14 = (pred[256]{0:T(512)(128)(4,1)S(1)}, pred[256]{0:T(512)(128)(4,1)}, u32[]{:S(2)}) copy-start(pred[256]{0:T(512)(128)(4,1)} %get-tuple-element.83) | copy-start | bytes 772
  98.5 9.4 %copy-start.15 = (pred[256]{0:T(512)(128)(4,1)S(1)}, pred[256]{0:T(512)(128)(4,1)}, u32[]{:S(2)}) copy-start(pred[256]{0:T(512)(128)(4,1)} %get-tuple-element.84) | copy-start | bytes 772
  98.5 9.4 %copy-start.16 = (pred[256]{0:T(512)(128)(4,1)S(1)}, pred[256]{0:T(512)(128)(4,1)}, u32[]{:S(2)}) copy-start(pred[256]{0:T(512)(128)(4,1)} %get-tuple-element.85) | copy-start | bytes 772
  98.5 9.4 %copy-start.17 = (pred[256]{0:T(512)(128)(4,1)S(1)}, pred[256]{0:T(512)(128)(4,1)}, u32[]{:S(2)}) copy-start(pred[256]{0:T(512)(128)(4,1)} %get-tuple-element.86) | copy-start | bytes 772
  98.5 9.4 %copy-start.18 = (pred[256]{0:T(512)(128)(4,1)S(1)}, pred[256]{0:T(512)(128)(4,1)}, u32[]{:S(2)}) copy-start(pred[256]{0:T(512)(128)(4,1)} %get-tuple-element.87) | copy-start | bytes 772
  98.5 9.4 %copy-start.19 = (pred[256]{0:T(512)(128)(4,1)S(1)}, pred[256]{0:T(512)(128)(4,1)}, u32[]{:S(2)}) copy-start(pred[256]{0:T(512)(128)(4,1)} %get-tuple-element.88) | copy-start | bytes 772
  98.5 9.4 %copy-start.20 = (pred[256]{0:T(512)(128)(4,1)S(1)}, pred[256]{0:T(512)(128)(4,1)}, u32[]{:S(2)}) copy-start(pred[256]{0:T(512)(128)(4,1)} %get-tuple-element.89) | copy-start | bytes 772
  98.6 9.4 %copy-start.21 = (pred[256]{0:T(512)(128)(4,1)S(1)}, pred[256]{0:T(512)(128)(4,1)}, u32[]{:S(2)}) copy-start(pred[256]{0:T(512)(128)(4,1)} %get-tuple-element.90) | copy-start | bytes 772
  98.6 9.4 %copy-start.22 = (pred[256]{0:T(512)(128)(4,1)S(1)}, pred[256]{0:T(512)(128)(4,1)}, u32[]{:S(2)}) copy-start(pred[256]{0:T(512)(128)(4,1)} %get-tuple-element.91) | copy-start | bytes 772
  99.8 3.7 %collective-permute-start = (bf16[15,1024]{1,0:T(8,128)(2,1)S(1)}, bf16[15,1024]{1,0:T(8,128)(2,1)S(1)}, u32[]{:S(2)}, u32[]{:S(2)}) collective-permute-start(bf16[15,1024]{1,0:T(8,128)(2,1)S(1)} %get-tuple-element.41), channel_id=1, source_target_pairs={{0,1},{1,2},{2,3},{4,5},{5,6},{6,7},{8,9},{9,10},{10,11},{12,13},{... | collective-permute-start | bytes 92168 | tf_op jit(solution)/shard_map/ppermute | solution.py:22
  101.9 5.8 %collective-permute-start.1 = (bf16[15,1024]{1,0:T(8,128)(2,1)S(1)}, bf16[15,1024]{1,0:T(8,128)(2,1)S(1)}, u32[]{:S(2)}, u32[]{:S(2)}) collective-permute-start(bf16[15,1024]{1,0:T(8,128)(2,1)S(1)} %get-tuple-element.42), channel_id=1, source_target_pairs={{1,0},{2,1},{3,2},{5,4},{6,5},{7,6},{9,8},{10,9},{11,10},{13,12},{... | collective-permute-start | bytes 92168 | tf_op jit(solution)/shard_map/ppermute | solution.py:25
  (7 other events, 52.6 us)
Sparse Core Ops, SparseCore 0:
  36.8 44.7 all-gather.1
where the time goes:
time: 122 us
  waiting for transfers between devices  54.3 us (45%)
  local copies, waits for them, and re-layouts  18.6 us (15%)
  other arithmetic  15.6 us (13%)
  between operations  14 us (11%)
  starting transfers between devices  9.73 us (8%)
  matrix products  9.73 us (8%)
    all_gather x1, waiting for transfers between devices, per_device(): fetched = lax.all_gather(key_value, 'ctx', axis=1, tiled=True)  35.4 us
    all_to_all x1, waiting for transfers between devices, per_device(): lax.all_to_all(outgoing, 'ctx', split_axis=0, concat_axis=0, tiled=True)  14.4 us
    convert_element_type x1, other arithmetic, per_device(): (residual.astype(jnp.float32) + activation * jax.nn.sigmoid(activation))....  7.03 us
    all_to_all x1, starting transfers between devices, per_device(): lax.all_to_all(outgoing, 'ctx', split_axis=0, concat_axis=0, tiled=True)  6.35 us
    gather x2, local copies, waits for them, and re-layouts, local_utt(): picked = jnp.take(row_utt, jnp.clip(positions, 0, total_rows - 1), axis=0)  6.22 us
    ppermute x1, waiting for transfers between devices, extended_2(): lax.ppermute(lax.slice_in_dim(block, 0, width, axis=dim), axis, backward)  4.23 us
    dot_general x1, matrix products, attend(): jnp.einsum('hqk,khd->hqd', weights.astype(jnp.bfloat16), value_block, pre...  3.63 us
    slice x1, local copies, waits for them, and re-layouts, block_update(): key_block = block_pair[0].reshape(rows_here, HEADS, HEAD_DIM)  3.01 us
  transfers between devices with their start and end apart: 4, of which 4 were waited for; matrix products, arithmetic and copies ran while one was open for 8% of the time, Pallas kernels for 0%

commit v1 on v0

v1 whole, which is shorter than its diff:
```python
import functools
import math

import jax
import jax.numpy as jnp
from jax import lax
from jax.experimental import pallas as pl
from jax.experimental.pallas import tpu as pltpu
from jax.sharding import PartitionSpec as P

HEADS = 4
HEAD_DIM = 128
KERNEL = 31
TILE = 16
NEGATIVE = -1e30

VMEM = pl.BlockSpec(memory_space=pltpu.VMEM)
SMEM = pl.BlockSpec(memory_space=pltpu.SMEM)
ANY = pl.BlockSpec(memory_space=pl.ANY)


def layer_norm(rows):
    values = rows.astype(jnp.float32)
    center = values - jnp.mean(values, axis=-1, keepdims=True)
    spread = jnp.mean(center * center, axis=-1, keepdims=True)
    return center * lax.rsqrt(spread + 1e-05)


def key_value_kernel(rows_ref, key_weight_ref, value_weight_ref, key_ref, value_ref):
    normed = layer_norm(rows_ref[...]).astype(jnp.bfloat16)
    key_ref[...] = jnp.dot(
        normed, key_weight_ref[...], preferred_element_type=jnp.float32
    ).astype(jnp.bfloat16)
    value_ref[...] = jnp.dot(
        normed, value_weight_ref[...], preferred_element_type=jnp.float32
    ).astype(jnp.bfloat16)


def key_value(rows, key_weight, value_weight):
    shape = jax.ShapeDtypeStruct((rows.shape[0], key_weight.shape[1]), jnp.bfloat16)
    flops = 4 * rows.shape[0] * rows.shape[1] * key_weight.shape[1]
    return pl.pallas_call(
        key_value_kernel,
        out_shape=(shape, shape),
        in_specs=[VMEM] * 3,
        out_specs=(VMEM, VMEM),
        cost_estimate=pl.CostEstimate(flops=flops, bytes_accessed=3 << 20, transcendentals=0),
        name="key_value",
    )(rows, key_weight, value_weight)


def block_kernel(count, me_ref, source_ref, utt_ref, key_utt_ref, *refs):
    chunks = refs[:count]
    keys = refs[count : 2 * count]
    values = refs[2 * count : 3 * count]
    query_weight, output_weight, taps, scale, shift, out_ref = refs[3 * count : 3 * count + 6]
    grouped, query_utt, residual_rows, shaped_rows, sems = refs[3 * count + 6 :]
    me = me_ref[0]
    rows_dev = out_ref.shape[0]
    tiles_dev = rows_dev // TILE
    held = tiles_dev + 2
    total = tiles_dev * count
    first = me * tiles_dev - 1

    def tile_at(i):
        return jnp.clip(first + i, 0, total - 1)

    for i in range(held):
        source = source_ref[tile_at(i)]
        shard = source // tiles_dev
        row = pl.multiple_of((source % tiles_dev) * TILE, TILE)
        behind = lax.rem(me - shard + count, count)
        for step in range(count):

            @pl.when(behind == step)
            def _(step=step, row=row, i=i):
                pltpu.make_async_copy(
                    chunks[step].at[pl.ds(row, TILE), :],
                    grouped.at[pl.ds(i * TILE, TILE), :],
                    sems.at[i],
                ).start()

        query_utt[pl.ds(i * TILE, TILE), :] = jnp.full((TILE, 128), utt_ref[tile_at(i)], jnp.int32)
    for i in range(held):
        pltpu.make_async_copy(
            chunks[0].at[pl.ds(0, TILE), :], grouped.at[pl.ds(i * TILE, TILE), :], sems.at[i]
        ).wait()
    normed = layer_norm(grouped[...]).astype(jnp.bfloat16)
    queries = jnp.dot(normed, query_weight[...], preferred_element_type=jnp.float32).astype(
        jnp.bfloat16
    )
    allowed = query_utt[:, :1] == key_utt_ref[...]
    exponent_scale = math.log2(math.e) / math.sqrt(HEAD_DIM)
    heads = []
    for head in range(HEADS):
        columns = slice(head * HEAD_DIM, (head + 1) * HEAD_DIM)
        key_head = jnp.concatenate([key[:, columns] for key in keys], axis=0)
        value_head = jnp.concatenate([value[:, columns] for value in values], axis=0)
        scores = lax.dot_general(
            queries[:, columns],
            key_head,
            (((1,), (1,)), ((), ())),
            preferred_element_type=jnp.float32,
        )
        scores = jnp.where(allowed, scores, NEGATIVE)
        top = jnp.max(scores, axis=-1, keepdims=True)
        weights = jnp.exp2((scores - top) * exponent_scale)
        row_sum = jnp.sum(weights, axis=-1, keepdims=True)
        summed = jnp.dot(
            weights.astype(jnp.bfloat16), value_head, preferred_element_type=jnp.float32
        )
        heads.append((summed / row_sum).astype(jnp.bfloat16))
    attended = jnp.concatenate(heads, axis=1)
    residual = (
        grouped[...].astype(jnp.float32)
        + jnp.dot(attended, output_weight[...], preferred_element_type=jnp.float32)
    ).astype(jnp.bfloat16)
    residual_rows[...] = residual
    shaped_rows[...] = layer_norm(residual).astype(jnp.bfloat16).astype(jnp.float32)

    def one_tile(i, carried):
        here = utt_ref[tile_at(i + 1)]
        before = jnp.where((first + i >= 0) & (utt_ref[tile_at(i)] == here), 1.0, 0.0)
        after = jnp.where((first + i + 2 < total) & (utt_ref[tile_at(i + 2)] == here), 1.0, 0.0)
        row = pl.multiple_of(i * TILE, TILE)
        for block in range(out_ref.shape[1] // 128):
            columns = slice(block * 128, (block + 1) * 128)
            window = [
                shaped_rows[pl.ds(row, TILE), columns] * before,
                shaped_rows[pl.ds(row + TILE, TILE), columns],
                shaped_rows[pl.ds(row + 2 * TILE, TILE), columns] * after,
            ]
            window = jnp.concatenate(window, axis=0)
            convolved = None
            for part in range(8):
                total_part = None
                for start in range(0, 32, 8):
                    tap = start + part - 1
                    if tap < 0:
                        continue
                    term = window[start : start + 24] * taps[tap : tap + 1, columns]
                    total_part = term if total_part is None else total_part + term
                if part:
                    total_part = pltpu.roll(total_part, 24 - part, axis=0)
                total_part = total_part[:TILE]
                convolved = total_part if convolved is None else convolved + total_part
            activation = convolved * scale[:, columns] + shift[:, columns]
            kept = residual_rows[pl.ds(row + TILE, TILE), columns].astype(jnp.float32)
            out_ref[pl.ds(row, TILE), columns] = (
                kept + activation / (1.0 + jnp.exp(-activation))
            ).astype(jnp.bfloat16)
        return carried

    lax.fori_loop(0, tiles_dev, one_tile, 0)


def per_device(
    frames,
    tile_source,
    tile_utt,
    query_weight,
    key_weight,
    value_weight,
    output_weight,
    depth_weight,
    bn_scale,
    bn_shift,
):
    count = lax.axis_size("ctx")
    me = lax.axis_index("ctx")
    rows_dev, width = frames.shape
    tiles_dev = rows_dev // TILE
    ring = [(i, (i + 1) % count) for i in range(count)]
    chunks = [frames]
    for _ in range(count - 1):
        chunks.append(lax.ppermute(chunks[-1], "ctx", ring))
    pairs = [key_value(chunk, key_weight, value_weight) for chunk in chunks]
    shards = lax.rem(me - jnp.arange(count, dtype=jnp.int32) + count, count)
    arrived = (shards[:, None] * tiles_dev + jnp.arange(tiles_dev, dtype=jnp.int32)).reshape(-1)
    key_utt = jnp.sum(jnp.where(arrived[:, None] == tile_source[None, :], tile_utt[None, :], 0), axis=1)
    key_utt = jnp.repeat(key_utt, TILE).reshape(1, -1)
    held_rows = rows_dev + 2 * TILE
    return pl.pallas_call(
        functools.partial(block_kernel, count),
        out_shape=jax.ShapeDtypeStruct((rows_dev, width), jnp.bfloat16),
        in_specs=[SMEM] * 3 + [VMEM] + [ANY] * count + [VMEM] * (2 * count + 5),
        out_specs=VMEM,
        scratch_shapes=[
            pltpu.VMEM((held_rows, width), jnp.bfloat16),
            pltpu.VMEM((held_rows, 128), jnp.int32),
            pltpu.VMEM((held_rows, width), jnp.bfloat16),
            pltpu.VMEM((held_rows, width), jnp.float32),
            pltpu.SemaphoreType.DMA((tiles_dev + 2,)),
        ],
        cost_estimate=pl.CostEstimate(
            flops=2 << 30, bytes_accessed=8 << 20, transcendentals=1 << 20
        ),
        name="block",
    )(
        me.reshape(1),
        tile_source,
        tile_utt,
        key_utt,
        *chunks,
        *[pair[0] for pair in pairs],
        *[pair[1] for pair in pairs],
        query_weight,
        output_weight,
        depth_weight,
        bn_scale.reshape(1, -1),
        bn_shift.reshape(1, -1),
    )


def solution(mesh):
    return jax.shard_map(
        per_device,
        mesh=mesh,
        in_specs=(P(("dp", "ctx"), None), P("dp"), P("dp"), P(), P(), P(), P(), P(), P(), P()),
        out_specs=P(("dp", "ctx"), None),
        check_vma=False,
    )
```

time: 122 us -> 62.8 us (0.51)
  Pallas kernels: 0 us -> 25.5 us
  waiting for transfers between devices: 54.3 us -> 31.2 us
  local copies, waits for them, and re-layouts: 18.6 us -> 2.36 us
  other arithmetic: 15.6 us -> 0.25 us
  between operations: 14 us -> 0.02 us
  matrix products: 9.73 us -> 0 us
  starting transfers between devices: 9.73 us -> 3.06 us
    all_gather x1 -> x0, waiting for transfers between devices: 35.4 us -> none  [per_device(): fetched = lax.all_gather(key_value, 'ctx', axis=1, tiled=True)]
    ppermute x2 -> x3, waiting for transfers between devices: 4.42 us -> 31.2 us  [per_device(): chunks.append(lax.ppermute(chunks[-1], 'ctx', ring))]
    pallas_call x0 -> x5, Pallas kernels: none -> 25.5 us  [the longest x4 13.4 us: key_value(): pl.pallas_call(key_value_kernel, out_shape=(shape, shape), in_specs=[VMEM...]
    all_to_all x1 -> x0, waiting for transfers between devices: 14.4 us -> none  [per_device(): lax.all_to_all(outgoing, 'ctx', split_axis=0, concat_axis=0, tiled=True)]
    dot_general x6 -> x0, matrix products: 9.73 us -> none  [the longest x1 3.63 us: attend(): jnp.einsum('hqk,khd->hqd', weights.astype(jnp.bfloat16), value_block, pre...]
    gather x4 -> x0, local copies, waits for them, and re-layouts: 8.42 us -> none  [the longest x2 6.22 us: local_utt(): picked = jnp.take(row_utt, jnp.clip(positions, 0, total_rows - 1), axis=0)]
    convert_element_type x5 -> x0, other arithmetic: 7.82 us -> none  [the longest x1 7.03 us: per_device(): (residual.astype(jnp.float32) + activation * jax.nn.sigmoid(activation))....]
    all_to_all x1 -> x0, starting transfers between devices: 6.35 us -> none  [per_device(): lax.all_to_all(outgoing, 'ctx', split_axis=0, concat_axis=0, tiled=True)]
  transfers between devices with their start and end apart: 4 -> 3, of which waited for: 4 -> 3; matrix products, arithmetic and copies ran while one was open for 8% -> 2% of each run, Pallas kernels for 0% -> 16%
where the time goes in v1:
time: 62.8 us; the launch traced here: 62.4 us
  waiting for transfers between devices  31.2 us (50%)
  Pallas kernels  25.5 us (41%)
  starting transfers between devices  3.06 us (5%)
  local copies, waits for them, and re-layouts  2.36 us (4%)
    ppermute x3, waiting for transfers between devices, per_device(): chunks.append(lax.ppermute(chunks[-1], 'ctx', ring))  31.2 us
    pallas_call x4, Pallas kernels, key_value(): pl.pallas_call(key_value_kernel, out_shape=(shape, shape), in_specs=[VMEM...  13.4 us
    pallas_call x1, Pallas kernels, per_device(): pl.pallas_call(functools.partial(block_kernel, count), out_shape=jax.Shap...  12.1 us
    ppermute x3, starting transfers between devices, per_device(): chunks.append(lax.ppermute(chunks[-1], 'ctx', ring))  3.06 us
    unnamed x10, local copies, waits for them, and re-layouts  1.51 us
  transfers between devices with their start and end apart: 3, of which 3 were waited for; matrix products, arithmetic and copies ran while one was open for 2% of the time, Pallas kernels for 16%

profile of v1, /device:TPU:0, one launch (start us, length us, event | category | flops | bytes accessed | tf_op | source)
XLA Modules:
  0.0 62.4 jit_solution(11849410384900054624)
XLA Ops:
  0.0 3.1 %collective-permute-start = (bf16[256,1024]{1,0:T(8,128)(2,1)}, bf16[256,1024]{1,0:T(8,128)(2,1)S(1)}, u32[]{:S(2)}, u32[]{:S(2)}) collective-permute-start(bf16[256,1024]{1,0:T(8,128)(2,1)} %refs_0_.1), channel_id=1, source_target_pairs={{0,1},{1,2},{2,3},{3,0},{4,5},{5,6},{6,7},{7,4},{8,9},{9,10},{10,1... | collective-permute-start | bytes 1572872 | tf_op jit(solution)/shard_map/ppermute | solution.py:176
  3.1 14.2 %collective-permute-done.rows_ref.refs_1_ = bf16[256,1024]{1,0:T(8,128)(2,1)S(1)} collective-permute-done((bf16[256,1024]{1,0:T(8,128)(2,1)}, bf16[256,1024]{1,0:T(8,128)(2,1)S(1)}, u32[]{:S(2)}, u32[]{:S(2)}) %collective-permute-start) | collective-permute-done | bytes 524320 | tf_op jit(solution)/shard_map/ppermute | solution.py:176
  17.2 0.0 copy-start
  17.2 0.0 collective-permute-start.1
  17.2 14.9 %collective-permute-done.1.rows_ref.refs_2_ = bf16[256,1024]{1,0:T(8,128)(2,1)S(1)} collective-permute-done((bf16[256,1024]{1,0:T(8,128)(2,1)S(1)}, bf16[256,1024]{1,0:T(8,128)(2,1)S(1)}, u32[]{:S(2)}, u32[]{:S(2)}) %collective-permute-start.1) | collective-permute-done | bytes 524320 | tf_op jit(solution)/shard_map/ppermute | solution.py:176
  32.1 0.0 collective-permute-start.2
  32.1 0.1 iota_add_fusion
  32.2 0.0 copy-start.4
  32.2 0.1 add.31
  32.3 0.6 copy-done.3
  32.9 0.1 copy-done.4
  33.0 0.2 select_reduce_fusion
  33.1 0.1 broadcast_in_dim.21
  33.2 0.7 %reshape_reshape.3.key_utt_ref = s32[1,1024]{1,0:T(1,128)} reshape(s32[64,16]{1,0:T(8,128)S(1)} %broadcast_in_dim.21) | data formatting | bytes 8192 | tf_op jit(solution)/shard_map/reshape;reshape | solution.py:181
  33.9 3.4 %key_value.4 = (bf16[256,512]{1,0:T(8,128)(2,1)}, bf16[256,512]{1,0:T(8,128)(2,1)}) custom-call(bf16[256,1024]{1,0:T(8,128)(2,1)} %refs_0_.1, bf16[1024,512]{1,0:T(8,128)(2,1)} %key_weight_ref.7, bf16[1024,512]{1,0:T(8,128)(2,1)} %value_weight_ref.7), custom_call_target="tpu_custom_call" | custom-call | flops 536870912 | bytes 3145728 | tf_op jit(solution)/shard_map/key_value/pallas_call | solution.py:42
  37.2 0.0 copy-done
  37.3 0.0 copy-done.1
  37.3 3.3 %key_value.5 = (bf16[256,512]{1,0:T(8,128)(2,1)}, bf16[256,512]{1,0:T(8,128)(2,1)}) custom-call(bf16[256,1024]{1,0:T(8,128)(2,1)} %copy-done, bf16[1024,512]{1,0:T(8,128)(2,1)} %key_weight_ref.7, bf16[1024,512]{1,0:T(8,128)(2,1)} %value_weight_ref.7), custom_call_target="tpu_custom_call" | custom-call | flops 536870912 | bytes 3145728 | tf_op jit(solution)/shard_map/key_value/pallas_call | solution.py:42
  40.6 3.4 %key_value.6 = (bf16[256,512]{1,0:T(8,128)(2,1)}, bf16[256,512]{1,0:T(8,128)(2,1)}) custom-call(bf16[256,1024]{1,0:T(8,128)(2,1)} %copy-done.1, bf16[1024,512]{1,0:T(8,128)(2,1)} %key_weight_ref.7, bf16[1024,512]{1,0:T(8,128)(2,1)} %value_weight_ref.7), custom_call_target="tpu_custom_call" | custom-call | flops 536870912 | bytes 3145728 | tf_op jit(solution)/shard_map/key_value/pallas_call | solution.py:42
  44.0 2.2 %collective-permute-done.2.rows_ref.refs_3_ = bf16[256,1024]{1,0:T(8,128)(2,1)S(1)} collective-permute-done((bf16[256,1024]{1,0:T(8,128)(2,1)S(1)}, bf16[256,1024]{1,0:T(8,128)(2,1)S(1)}, u32[]{:S(2)}, u32[]{:S(2)}) %collective-permute-start.2) | collective-permute-done | bytes 524320 | tf_op jit(solution)/shard_map/ppermute | solution.py:176
  46.1 0.0 copy-start.2
  46.1 0.8 %copy-done.2 = bf16[256,1024]{1,0:T(8,128)(2,1)} copy-done((bf16[256,1024]{1,0:T(8,128)(2,1)}, bf16[256,1024]{1,0:T(8,128)(2,1)S(1)}, u32[]{:S(2)}) %copy-start.2) | copy-done | bytes 524312
  47.0 3.3 %key_value.7 = (bf16[256,512]{1,0:T(8,128)(2,1)}, bf16[256,512]{1,0:T(8,128)(2,1)}) custom-call(bf16[256,1024]{1,0:T(8,128)(2,1)} %copy-done.2, bf16[1024,512]{1,0:T(8,128)(2,1)} %key_weight_ref.7, bf16[1024,512]{1,0:T(8,128)(2,1)} %value_weight_ref.7), custom_call_target="tpu_custom_call" | custom-call | flops 536870912 | bytes 3145728 | tf_op jit(solution)/shard_map/key_value/pallas_call | solution.py:42
  50.3 12.1 %block.1 = bf16[256,1024]{1,0:T(8,128)(2,1)} custom-call(s32[1]{0:T(128)} %bitcast.me_ref, s32[64]{0:T(128)} %source_ref.1, s32[64]{0:T(128)} %utt_ref.1, s32[1,1024]{1,0:T(1,128)} %reshape_reshape.3.key_utt_ref, bf16[256,1024]{1,0:T(8,128)(2,1)} %refs_0_.1, bf16[256,1024]{1,0:T(8,128)(2,1)} %copy-done, bf16[256,1024]{1,0:T(8,128)(2,1)} %copy-done.1, ...), custom_call_target="tpu_custom_call" | custom-call | flops 2147483648 | bytes 8388608 | tf_op jit(solution)/shard_map/block/pallas_call | solution.py:183
  (3 shorter events, 0.0 us)
Async XLA Ops:
  0.0 17.2 %collective-permute-start = (bf16[256,1024]{1,0:T(8,128)(2,1)}, bf16[256,1024]{1,0:T(8,128)(2,1)S(1)}, u32[]{:S(2)}, u32[]{:S(2)}) collective-permute-start(bf16[256,1024]{1,0:T(8,128)(2,1)} %refs_0_.1), channel_id=1, source_target_pairs={{0,1},{1,2},{2,3},{3,0},{4,5},{5,6},{6,7},{7,4},{8,9},{9,10},{10,1... | collective-permute-start | bytes 1572872 | tf_op jit(solution)/shard_map/ppermute | solution.py:176
  17.2 20.0 %copy-start = (bf16[256,1024]{1,0:T(8,128)(2,1)}, bf16[256,1024]{1,0:T(8,128)(2,1)S(1)}, u32[]{:S(2)}) copy-start(bf16[256,1024]{1,0:T(8,128)(2,1)S(1)} %collective-permute-done.rows_ref.refs_1_) | copy-start | bytes 1572868
  17.2 14.9 %collective-permute-start.1 = (bf16[256,1024]{1,0:T(8,128)(2,1)S(1)}, bf16[256,1024]{1,0:T(8,128)(2,1)S(1)}, u32[]{:S(2)}, u32[]{:S(2)}) collective-permute-start(bf16[256,1024]{1,0:T(8,128)(2,1)S(1)} %collective-permute-done.rows_ref.refs_1_), channel_id=1, source_target_pairs={{0,1},{1,2},{2,3},{3,0},{4,5},{5,6},{6,7},{7,4},{8,9},{9,10},{10,1... | collective-permute-start | bytes 1572872 | tf_op jit(solution)/shard_map/ppermute | solution.py:176
  32.1 5.2 %copy-start.1 = (bf16[256,1024]{1,0:T(8,128)(2,1)}, bf16[256,1024]{1,0:T(8,128)(2,1)S(1)}, u32[]{:S(2)}) copy-start(bf16[256,1024]{1,0:T(8,128)(2,1)S(1)} %collective-permute-done.1.rows_ref.refs_2_) | copy-start | bytes 1572868
  32.1 14.0 %collective-permute-start.2 = (bf16[256,1024]{1,0:T(8,128)(2,1)S(1)}, bf16[256,1024]{1,0:T(8,128)(2,1)S(1)}, u32[]{:S(2)}, u32[]{:S(2)}) collective-permute-start(bf16[256,1024]{1,0:T(8,128)(2,1)S(1)} %collective-permute-done.1.rows_ref.refs_2_), channel_id=1, source_target_pairs={{0,1},{1,2},{2,3},{3,0},{4,5},{5,6},{6,7},{7,4},{8,9},{9,10},{10,1... | collective-permute-start | bytes 1572872 | tf_op jit(solution)/shard_map/ppermute | solution.py:176
  32.2 0.7 %copy-start.3 = (s32[64]{0:T(128)S(1)}, s32[64]{0:T(128)}, u32[]{:S(2)}) copy-start(s32[64]{0:T(128)} %source_ref.1) | copy-start | bytes 772
  32.2 0.8 %copy-start.4 = (s32[64]{0:T(128)S(1)}, s32[64]{0:T(128)}, u32[]{:S(2)}) copy-start(s32[64]{0:T(128)} %utt_ref.1) | copy-start | bytes 772
  46.1 0.8 %copy-start.2 = (bf16[256,1024]{1,0:T(8,128)(2,1)}, bf16[256,1024]{1,0:T(8,128)(2,1)S(1)}, u32[]{:S(2)}) copy-start(bf16[256,1024]{1,0:T(8,128)(2,1)S(1)} %collective-permute-done.2.rows_ref.refs_3_) | copy-start | bytes 1572868

commit v2 on v1

v2 whole, which is shorter than its diff:
```python
import functools
import math

import jax
import jax.numpy as jnp
from jax import lax
from jax.experimental import pallas as pl
from jax.experimental.pallas import tpu as pltpu
from jax.sharding import PartitionSpec as P

HEADS = 4
HEAD_DIM = 128
KERNEL = 31
TILE = 16
UTTS = 4
NEGATIVE = -1e30

VMEM = pl.BlockSpec(memory_space=pltpu.VMEM)
SMEM = pl.BlockSpec(memory_space=pltpu.SMEM)


def params(mib):
    return pltpu.CompilerParams(vmem_limit_bytes=mib << 20)


def layer_norm(rows):
    values = rows.astype(jnp.float32)
    center = values - jnp.mean(values, axis=-1, keepdims=True)
    spread = jnp.mean(center * center, axis=-1, keepdims=True)
    return center * lax.rsqrt(spread + 1e-05)


def project(rows, weight_ref):
    return jnp.dot(rows, weight_ref[...], preferred_element_type=jnp.float32).astype(jnp.bfloat16)


def attend_and_convolve(
    first,
    total,
    utt_ref,
    grouped,
    query_utt,
    key_utt,
    key_parts,
    value_parts,
    query_weight,
    output_weight,
    taps,
    scale,
    shift,
    out_ref,
    padded,
    residual_rows,
):
    rows_dev, width = out_ref.shape
    tiles_dev = rows_dev // TILE
    held = tiles_dev + 2

    def tile_at(i):
        return jnp.clip(first + i, 0, total - 1)

    padded[...] = jnp.zeros_like(padded)
    queries = project(layer_norm(grouped[...]).astype(jnp.bfloat16), query_weight)
    allowed = query_utt[:, :1] == key_utt
    exponent_scale = math.log2(math.e) / math.sqrt(HEAD_DIM)
    heads = []
    for head in range(HEADS):
        columns = slice(head * HEAD_DIM, (head + 1) * HEAD_DIM)
        key_head = jnp.concatenate([part[:, columns] for part in key_parts], axis=0)
        value_head = jnp.concatenate([part[:, columns] for part in value_parts], axis=0)
        scores = lax.dot_general(
            queries[:, columns],
            key_head,
            (((1,), (1,)), ((), ())),
            preferred_element_type=jnp.float32,
        )
        scores = jnp.where(allowed, scores, NEGATIVE)
        top = jnp.max(scores, axis=-1, keepdims=True)
        weights = jnp.exp2((scores - top) * exponent_scale)
        row_sum = jnp.sum(weights, axis=-1, keepdims=True)
        summed = jnp.dot(
            weights.astype(jnp.bfloat16), value_head, preferred_element_type=jnp.float32
        )
        heads.append((summed / row_sum).astype(jnp.bfloat16))
    attended = jnp.concatenate(heads, axis=1)
    residual = (
        grouped[...].astype(jnp.float32)
        + jnp.dot(attended, output_weight[...], preferred_element_type=jnp.float32)
    ).astype(jnp.bfloat16)
    residual_rows[...] = residual[TILE : TILE + rows_dev]
    shaped = layer_norm(residual).astype(jnp.bfloat16).astype(jnp.float32)
    places = []
    place = jnp.int32(1)
    for i in range(held):
        if i:
            place = place + 1
            place = place + jnp.where(utt_ref[tile_at(i)] == utt_ref[tile_at(i - 1)], 0, 1)
        inside = (first + i >= 0) & (first + i < total)
        target = jnp.where(inside, place, padded.shape[1] // TILE - 1)
        row = pl.multiple_of(target * TILE, TILE)
        for block in range(width // 128):
            padded[block, pl.ds(row, TILE), :] = shaped[
                i * TILE : (i + 1) * TILE, block * 128 : (block + 1) * 128
            ]
        places.append(place)

    def one_tile(i, place):
        gap = jnp.where(utt_ref[tile_at(i + 1)] == utt_ref[tile_at(i)], 0, 1)
        place = place + 1 + gap
        start = pl.multiple_of(place * TILE, TILE)
        row = pl.multiple_of(i * TILE, TILE)
        for block in range(width // 128):
            columns = slice(block * 128, (block + 1) * 128)
            sums = [None] * 4
            for tap in range(KERNEL):
                term = (
                    padded[block, pl.ds(start + (tap - KERNEL // 2), TILE), :]
                    * taps[tap : tap + 1, columns]
                )
                sums[tap % 4] = term if sums[tap % 4] is None else sums[tap % 4] + term
            convolved = (sums[0] + sums[1]) + (sums[2] + sums[3])
            half = 0.5 * (convolved * scale[:, columns] + shift[:, columns])
            kept = residual_rows[pl.ds(row, TILE), columns].astype(jnp.float32)
            out_ref[pl.ds(row, TILE), columns] = (kept + (half + half * jnp.tanh(half))).astype(
                jnp.bfloat16
            )
        return place

    lax.fori_loop(0, tiles_dev, one_tile, places[0], unroll=2)


def padded_rows(tiles_dev):
    return (1 + tiles_dev + 2 + (UTTS - 1) + 2) * TILE


def block_scratch(rows_dev, width):
    held_rows = rows_dev + 2 * TILE
    return [
        pltpu.VMEM((held_rows, width), jnp.bfloat16),
        pltpu.VMEM((held_rows, 128), jnp.int32),
        pltpu.VMEM((width // 128, padded_rows(rows_dev // TILE), 128), jnp.float32),
        pltpu.VMEM((rows_dev, width), jnp.bfloat16),
    ]


def key_value_kernel(rows_ref, key_weight_ref, value_weight_ref, key_ref, value_ref):
    normed = layer_norm(rows_ref[...]).astype(jnp.bfloat16)
    key_ref[...] = project(normed, key_weight_ref)
    value_ref[...] = project(normed, value_weight_ref)


def key_value(rows, key_weight, value_weight):
    shape = jax.ShapeDtypeStruct((rows.shape[0], key_weight.shape[1]), jnp.bfloat16)
    flops = 4 * rows.shape[0] * rows.shape[1] * key_weight.shape[1]
    return pl.pallas_call(
        key_value_kernel,
        out_shape=(shape, shape),
        in_specs=[VMEM] * 3,
        out_specs=(VMEM, VMEM),
        cost_estimate=pl.CostEstimate(flops=flops, bytes_accessed=3 << 20, transcendentals=0),
        name="key_value",
    )(rows, key_weight, value_weight)


def ring_kernel(count, me_ref, source_ref, utt_ref, key_utt_ref, *refs):
    chunks = refs[:count]
    keys = refs[count : 2 * count]
    values = refs[2 * count : 3 * count]
    weights_and_out = refs[3 * count : 3 * count + 6]
    grouped, query_utt, padded, residual_rows, sems = refs[3 * count + 6 :]
    me = me_ref[0]
    tiles_dev = weights_and_out[-1].shape[0] // TILE
    held = tiles_dev + 2
    total = tiles_dev * count
    first = me * tiles_dev - 1
    for i in range(held):
        position = jnp.clip(first + i, 0, total - 1)
        source = source_ref[position]
        row = pl.multiple_of((source % tiles_dev) * TILE, TILE)
        behind = lax.rem(me - source // tiles_dev + count, count)
        for step in range(count):

            @pl.when(behind == step)
            def _(step=step, row=row, i=i):
                pltpu.make_async_copy(
                    chunks[step].at[pl.ds(row, TILE), :],
                    grouped.at[pl.ds(i * TILE, TILE), :],
                    sems.at[i],
                ).start()

        query_utt[pl.ds(i * TILE, TILE), :] = jnp.full((TILE, 128), utt_ref[position], jnp.int32)
    for i in range(held):
        pltpu.make_async_copy(
            chunks[0].at[pl.ds(0, TILE), :], grouped.at[pl.ds(i * TILE, TILE), :], sems.at[i]
        ).wait()
    attend_and_convolve(
        first, total, utt_ref, grouped, query_utt, key_utt_ref[...], keys, values,
        *weights_and_out, padded, residual_rows,
    )


def ring_block(
    frames, tile_source, tile_utt, query_weight, key_weight, value_weight, output_weight,
    depth_weight, bn_scale, bn_shift,
):
    count = lax.axis_size("ctx")
    me = lax.axis_index("ctx")
    rows_dev, width = frames.shape
    tiles_dev = rows_dev // TILE
    ring = [(i, (i + 1) % count) for i in range(count)]
    chunks = [frames]
    for _ in range(count - 1):
        chunks.append(lax.ppermute(chunks[-1], "ctx", ring))
    pairs = [key_value(chunk, key_weight, value_weight) for chunk in chunks]
    shards = lax.rem(me - jnp.arange(count, dtype=jnp.int32) + count, count)
    arrived = (shards[:, None] * tiles_dev + jnp.arange(tiles_dev, dtype=jnp.int32)).reshape(-1)
    key_utt = jnp.sum(
        jnp.where(arrived[:, None] == tile_source[None, :], tile_utt[None, :], 0), axis=1
    )
    key_utt = jnp.repeat(key_utt, TILE).reshape(1, -1)
    return pl.pallas_call(
        functools.partial(ring_kernel, count),
        out_shape=jax.ShapeDtypeStruct((rows_dev, width), jnp.bfloat16),
        in_specs=[SMEM] * 3
        + [VMEM]
        + [pl.BlockSpec(memory_space=pl.ANY)] * count
        + [VMEM] * (2 * count + 5),
        out_specs=VMEM,
        scratch_shapes=block_scratch(rows_dev, width)
        + [pltpu.SemaphoreType.DMA((tiles_dev + 2,))],
        cost_estimate=pl.CostEstimate(
            flops=2 << 30, bytes_accessed=8 << 20, transcendentals=1 << 20
        ),
        name="ring_block",
    )(
        me.reshape(1), tile_source, tile_utt, key_utt, *chunks,
        *[pair[0] for pair in pairs], *[pair[1] for pair in pairs],
        query_weight, output_weight, depth_weight, bn_scale.reshape(1, -1), bn_shift.reshape(1, -1),
    )


COUNT = 4
SWAP_OUTER = [(0, 1), (1, 0), (2, 3), (3, 2)]
SWAP_INNER = [(1, 2), (2, 1)]
TO_ENDS = [(1, 0), (2, 3)]
FROM_ENDS = [(0, 1), (3, 2)]


def quarter_of(source_shard, target):
    return jnp.where(source_shard % 2 == 1, target, COUNT - 1 - target)


def arrange_kernel(me_ref, source_ref, rows_ref, low_ref, last_ref, high_ref, start_ref, filled):
    me = me_ref[0]
    tiles_dev = rows_ref.shape[0] // TILE
    quarter_rows = rows_ref.shape[0] // COUNT
    for target in range(COUNT):
        filled[target] = 0

    def one(position, carried):
        source = source_ref[position]

        @pl.when(source // tiles_dev == me)
        def _():
            target = position // tiles_dev
            rank = filled[target]
            filled[target] = rank + 1
            quarter = quarter_of(me, target)
            tile = rows_ref[pl.ds(pl.multiple_of((source % tiles_dev) * TILE, TILE), TILE), :]
            row = pl.multiple_of(quarter * quarter_rows + rank * TILE, TILE)

            @pl.when(quarter < COUNT - 1)
            def _():
                low_ref[pl.ds(row, TILE), :] = tile

            @pl.when(quarter == COUNT - 1)
            def _():
                last_ref[pl.ds(pl.multiple_of(rank * TILE, TILE), TILE), :] = tile

            @pl.when(quarter > 0)
            def _():
                high_ref[pl.ds(pl.multiple_of(row - quarter_rows, TILE), TILE), :] = tile

            @pl.when(quarter == 0)
            def _():
                start_ref[pl.ds(row, TILE), :] = tile

        return carried

    lax.fori_loop(0, COUNT * tiles_dev, one, 0, unroll=4)


def tables_kernel(source_ref, utt_ref, rank_ref, key_utt_ref, filled):
    total = source_ref.shape[0]
    tiles_dev = total // COUNT
    per_pair = tiles_dev // COUNT
    for pair in range(COUNT * COUNT):
        filled[pair] = 0

    def one(position, carried):
        pair = (source_ref[position] // tiles_dev) * COUNT + position // tiles_dev
        rank = filled[pair]
        filled[pair] = rank + 1
        rank_ref[position] = rank
        key_utt_ref[pair * per_pair + rank] = utt_ref[position]
        return carried

    lax.fori_loop(0, total, one, 0, unroll=4)


def held_tiles(me_ref, source_ref, rank_ref, rows_dev):
    me = me_ref[0]
    tiles_dev = rows_dev // TILE
    total = tiles_dev * COUNT
    for i in range(tiles_dev + 2):
        position = jnp.clip(me * tiles_dev - 1 + i, 0, total - 1)
        source = source_ref[position] // tiles_dev
        quarter = quarter_of(source, position // tiles_dev)
        row = quarter * (rows_dev // COUNT) + rank_ref[position] * TILE
        yield i, me ^ source, quarter, row


def early_kernel(
    me_ref, source_ref, rank_ref,
    low, last, high, near, near_last, inner, inner_end,
    key_weight, value_weight, key_ref, value_ref, grouped, rows,
):
    me = me_ref[0]
    is_end = (me == 0) | (me == COUNT - 1)
    rows_dev = high.shape[0] + last.shape[0]
    piece = low.shape[0]
    quarter_rows = last.shape[0]
    rows[0:piece] = low[...]
    rows[piece:rows_dev] = last[...]
    base = rows_dev
    rows[base : base + piece] = near[...]

    @pl.when(is_end)
    def _():
        rows[base + piece : base + 2 * piece] = inner_end[...]

    @pl.when(jnp.logical_not(is_end))
    def _():
        rows[base + piece : base + 2 * piece] = inner[...]

    rows[base + 2 * piece :] = near_last[...]
    for i, apart, quarter, row in held_tiles(me_ref, source_ref, rank_ref, rows_dev):
        second = jnp.where(is_end, 2, 3)
        place = row
        place = jnp.where(
            apart == 1, jnp.where(quarter == 3, base + 2 * piece - 3 * quarter_rows, base) + row, place
        )
        place = jnp.where(apart == second, base + piece - quarter_rows + row, place)

        @pl.when((apart <= 1) | (apart == second))
        def _(i=i, place=place):
            grouped[i * TILE : (i + 1) * TILE] = rows[
                pl.ds(pl.multiple_of(place, TILE), TILE), :
            ]

    normed = layer_norm(rows[...]).astype(jnp.bfloat16)
    key_ref[...] = project(normed, key_weight)
    value_ref[...] = project(normed, value_weight)


def middle_kernel(me_ref, first, second, key_weight, value_weight, key_ref, value_ref):
    rows = jnp.concatenate([first[...], second[...]], axis=0)
    normed = layer_norm(rows).astype(jnp.bfloat16)
    key_ref[...] = project(normed, key_weight)
    value_ref[...] = project(normed, value_weight)


def final_kernel(
    me_ref, source_ref, utt_ref, rank_ref, key_utt_table,
    early_grouped, far, far_end, early_key, early_value, middle_key, middle_value,
    key_weight, value_weight, query_weight, output_weight, taps, scale, shift,
    out_ref, grouped, query_utt, padded, residual_rows, late,
):
    me = me_ref[0]
    is_end = (me == 0) | (me == COUNT - 1)
    rows_dev = out_ref.shape[0]
    tiles_dev = rows_dev // TILE
    total = tiles_dev * COUNT
    first = me * tiles_dev - 1
    per_pair = tiles_dev // COUNT

    @pl.when(is_end)
    def _():
        late[...] = far_end[...]

    @pl.when(jnp.logical_not(is_end))
    def _():
        late[...] = far[...]

    third = jnp.where(is_end, 3, 2)
    for i, apart, _, row in held_tiles(me_ref, source_ref, rank_ref, rows_dev):
        rows_of_tile = slice(i * TILE, (i + 1) * TILE)

        @pl.when(apart == third)
        def _(row=row, rows_of_tile=rows_of_tile):
            grouped[rows_of_tile] = late[pl.ds(pl.multiple_of(row, TILE), TILE), :]

        @pl.when(apart != third)
        def _(rows_of_tile=rows_of_tile):
            grouped[rows_of_tile] = early_grouped[rows_of_tile]

        query_utt[rows_of_tile, :] = jnp.full(
            (TILE, 128), utt_ref[jnp.clip(first + i, 0, total - 1)], jnp.int32
        )
    normed = layer_norm(late[...]).astype(jnp.bfloat16)
    late_key = project(normed, key_weight)
    late_value = project(normed, value_weight)

    near = me ^ 1
    second = me ^ jnp.where(is_end, 2, 3)
    far_shard = me ^ third
    order = [(me, quarter, False) for quarter in (0, 1, 2, 3)]
    order += [(near, quarter, False) for quarter in (0, 1, 2)]
    order += [(second, quarter, False) for quarter in (1, 2, 3)]
    order += [(near, 3, True), (second, 0, True), (far_shard, 3, True)]
    order += [(far_shard, quarter, False) for quarter in (0, 1, 2)]
    lane_tile = lax.broadcasted_iota(jnp.int32, (1, 128), 1) // TILE
    pieces = []
    tile_values = []
    for shard, quarter, inner_only in order:
        target = jnp.where(shard % 2 == 1, quarter, COUNT - 1 - quarter)
        for rank in range(per_pair):
            utt = key_utt_table[(shard * COUNT + target) * per_pair + rank]
            if inner_only:
                utt = jnp.where(is_end, -1, utt)
            tile_values.append(utt)
    per_vector = 128 // TILE
    for start in range(0, len(tile_values), per_vector):
        vector = jnp.full((1, 128), tile_values[start], jnp.int32)
        for k in range(1, per_vector):
            vector = jnp.where(lane_tile == k, tile_values[start + k], vector)
        pieces.append(vector)
    key_utt = jnp.concatenate(pieces, axis=1)
    attend_and_convolve(
        first, total, utt_ref, grouped, query_utt, key_utt,
        [early_key, middle_key, late_key], [early_value, middle_value, late_value],
        query_weight, output_weight, taps, scale, shift, out_ref, padded, residual_rows,
    )


def after(value, other):
    return lax.optimization_barrier((value, other))[0]


def line_block(
    frames, tile_source, tile_utt, query_weight, key_weight, value_weight, output_weight,
    depth_weight, bn_scale, bn_shift,
):
    me = lax.axis_index("ctx").reshape(1)
    rows_dev, width = frames.shape
    quarter = rows_dev // COUNT
    piece = rows_dev - quarter
    total = tile_source.shape[0]
    wide = key_weight.shape[1]

    def shape(rows, columns=width, kind=jnp.bfloat16):
        return jax.ShapeDtypeStruct((rows, columns), kind)

    def cost(rows):
        return pl.CostEstimate(
            flops=4 * rows * width * wide, bytes_accessed=rows * width * 4, transcendentals=rows
        )

    low, last, high, start = pl.pallas_call(
        arrange_kernel,
        out_shape=(shape(piece), shape(quarter), shape(piece), shape(quarter)),
        in_specs=[SMEM] * 2 + [VMEM],
        out_specs=(VMEM,) * 4,
        scratch_shapes=[pltpu.SMEM((COUNT,), jnp.int32)],
        compiler_params=params(8),
        name="arrange",
    )(me, tile_source, frames)
    swap = functools.partial(lax.ppermute, axis_name="ctx")
    near = swap(low, perm=SWAP_OUTER)
    inner = swap(high, perm=SWAP_INNER)
    rank, key_utt = pl.pallas_call(
        tables_kernel,
        out_shape=(jax.ShapeDtypeStruct((total,), jnp.int32),) * 2,
        in_specs=[SMEM] * 2,
        out_specs=(SMEM, SMEM),
        scratch_shapes=[pltpu.SMEM((COUNT * COUNT,), jnp.int32)],
        compiler_params=params(4),
        name="tables",
    )(tile_source, tile_utt)
    far = swap(near, perm=SWAP_INNER)
    inner_end = swap(inner, perm=TO_ENDS)
    near_last = swap(after(last, near), perm=FROM_ENDS)
    far_end = swap(far, perm=TO_ENDS)
    inner_start = swap(after(start, far), perm=SWAP_INNER)
    far_last = swap(after(near_last, far), perm=SWAP_INNER)

    early_rows = rows_dev + 2 * piece + quarter
    early_key, early_value, grouped = pl.pallas_call(
        early_kernel,
        out_shape=(shape(early_rows, wide), shape(early_rows, wide), shape(rows_dev + 2 * TILE)),
        in_specs=[SMEM] * 3 + [VMEM] * 9,
        out_specs=(VMEM,) * 3,
        scratch_shapes=[pltpu.VMEM((early_rows, width), jnp.bfloat16)],
        compiler_params=params(16),
        cost_estimate=cost(early_rows),
        name="early",
    )(
        me, tile_source, rank, low, last, high, near, near_last, inner, inner_end,
        key_weight, value_weight,
    )
    middle_key, middle_value = pl.pallas_call(
        middle_kernel,
        out_shape=(shape(2 * quarter, wide),) * 2,
        in_specs=[SMEM] + [VMEM] * 4,
        out_specs=(VMEM,) * 2,
        compiler_params=params(8),
        cost_estimate=cost(2 * quarter),
        name="middle",
    )(me, inner_start, far_last, key_weight, value_weight)
    return pl.pallas_call(
        final_kernel,
        out_shape=shape(rows_dev),
        in_specs=[SMEM] * 5 + [VMEM] * 14,
        out_specs=VMEM,
        scratch_shapes=block_scratch(rows_dev, width) + [pltpu.VMEM((piece, width), jnp.bfloat16)],
        compiler_params=params(28),
        cost_estimate=pl.CostEstimate(
            flops=2 << 30, bytes_accessed=8 << 20, transcendentals=1 << 20
        ),
        name="final",
    )(
        me, tile_source, tile_utt, rank, key_utt,
        grouped, far, far_end, early_key, early_value, middle_key, middle_value,
        key_weight, value_weight, query_weight, output_weight,
        depth_weight, bn_scale.reshape(1, -1), bn_shift.reshape(1, -1),
    )


def per_device(*arrays):
    tiles_dev = arrays[0].shape[0] // TILE
    if lax.axis_size("ctx") == COUNT and tiles_dev % COUNT == 0:
        return line_block(*arrays)
    return ring_block(*arrays)


def solution(mesh):
    return jax.shard_map(
        per_device,
        mesh=mesh,
        in_specs=(P(("dp", "ctx"), None), P("dp"), P("dp"), P(), P(), P(), P(), P(), P(), P()),
        out_specs=P(("dp", "ctx"), None),
        check_vma=False,
    )
```

time: 62.8 us -> 55.3 us (0.88)
  the two profiles are of different devices: /device:TPU:0 before, /device:TPU:8 now
where the time goes in v2:
time: 55.3 us; the launch traced here: 54.9 us
  starting transfers between devices  19.6 us (35%)
  Pallas kernels  17.4 us (31%)
  waiting for transfers between devices  12.8 us (23%)
  local copies, waits for them, and re-layouts  4.98 us (9%)
    pallas_call x1, Pallas kernels, line_block(): pl.pallas_call(final_kernel, out_shape=shape(rows_dev), in_specs=[SMEM] *...  9.48 us
    ppermute x1, waiting for transfers between devices, line_block(): far = swap(near, perm=SWAP_INNER)  7.07 us
    ppermute x1, waiting for transfers between devices, line_block(): near = swap(low, perm=SWAP_OUTER)  5.66 us
    ppermute x1, starting transfers between devices, line_block(): inner = swap(high, perm=SWAP_INNER)  5.16 us
    unnamed x24, local copies, waits for them, and re-layouts  4.98 us
    ppermute x1, starting transfers between devices, line_block(): inner_start = swap(after(start, far), perm=SWAP_INNER)  3.48 us
    ppermute x1, starting transfers between devices, line_block(): far_last = swap(after(near_last, far), perm=SWAP_INNER)  3.47 us
    ppermute x1, starting transfers between devices, line_block(): far = swap(near, perm=SWAP_INNER)  3.47 us
  transfers between devices with their start and end apart: 8, of which 2 were waited for; matrix products, arithmetic and copies ran while one was open for 0% of the time, Pallas kernels for 11%

profile of v2, /device:TPU:8, one launch (start us, length us, event | category | flops | bytes accessed | tf_op | source)
XLA Modules:
  0.0 54.9 jit_solution(11213236424158417215)
XLA Ops:
  0.0 0.7 %copy-done.5 = s32[64]{0:T(128)S(1)} copy-done((s32[64]{0:T(128)S(1)}, s32[64]{0:T(128)}, u32[]{:S(2)}) %copy-start.5) | copy-done | bytes 280
  0.7 1.0 %copy-done.4 = bf16[256,1024]{1,0:T(8,128)(2,1)S(1)} copy-done((bf16[256,1024]{1,0:T(8,128)(2,1)S(1)}, bf16[256,1024]{1,0:T(8,128)(2,1)}, u32[]{:S(2)}) %copy-start.4) | copy-done | bytes 524312
  1.7 2.0 %arrange.1 = (bf16[192,1024]{1,0:T(8,128)(2,1)S(1)}, bf16[64,1024]{1,0:T(8,128)(2,1)S(1)}, bf16[192,1024]{1,0:T(8,128)(2,1)S(1)}, bf16[64,1024]{1,0:T(8,128)(2,1)S(1)}) custom-call(s32[1]{0:T(128)} %bitcast.me_ref, s32[64]{0:T(128)S(1)} %copy-done.5, bf16[256,1024]{1,0:T(8,128)(2,1)S(1)} %copy-done.4), custom_call_target="tpu_custom_call" | custom-call | tf_op jit(solution)/shard_map/arrange/pallas_call | solution.py:469
  3.7 0.1 collective-permute-start
  3.8 5.2 %collective-permute-start.2 = (bf16[192,1024]{1,0:T(8,128)(2,1)S(1)}, bf16[192,1024]{1,0:T(8,128)(2,1)S(1)}, u32[]{:S(2)}, u32[]{:S(2)}) collective-permute-start(bf16[192,1024]{1,0:T(8,128)(2,1)S(1)} %get-tuple-element.23.high), channel_id=1, source_target_pairs={{1,2},{2,1},{5,6},{6,5},{9,10},{10,9},{13,14},{14,13},{17,18},{18,... | collective-permute-start | bytes 1179656 | tf_op jit(solution)/shard_map/ppermute | solution.py:480
  9.0 5.7 %collective-permute-done.near = bf16[192,1024]{1,0:T(8,128)(2,1)S(1)} collective-permute-done((bf16[192,1024]{1,0:T(8,128)(2,1)S(1)}, bf16[192,1024]{1,0:T(8,128)(2,1)S(1)}, u32[]{:S(2)}, u32[]{:S(2)}) %collective-permute-start) | collective-permute-done | bytes 393248 | tf_op jit(solution)/shard_map/ppermute | solution.py:479
  14.6 3.5 %collective-permute-start.4 = (bf16[192,1024]{1,0:T(8,128)(2,1)S(1)}, bf16[192,1024]{1,0:T(8,128)(2,1)S(1)}, u32[]{:S(2)}, u32[]{:S(2)}) collective-permute-start(bf16[192,1024]{1,0:T(8,128)(2,1)S(1)} %collective-permute-done.near), channel_id=1, source_target_pairs={{1,2},{2,1},{5,6},{6,5},{9,10},{10,9},{13,14},{14,13},{17,18},{18,... | collective-permute-start | bytes 1179656 | tf_op jit(solution)/shard_map/ppermute | solution.py:490
  18.1 1.3 %collective-permute-start.3 = (bf16[192,1024]{1,0:T(8,128)(2,1)S(1)}, bf16[192,1024]{1,0:T(8,128)(2,1)S(1)}, u32[]{:S(2)}, u32[]{:S(2)}) collective-permute-start(bf16[192,1024]{1,0:T(8,128)(2,1)S(1)} %collective-permute-done.2.inner), channel_id=1, source_target_pairs={{1,0},{2,3},{5,4},{6,7},{9,8},{10,11},{13,12},{14,15},{17,16},{18,... | collective-permute-start | bytes 1179656 | tf_op jit(solution)/shard_map/ppermute | solution.py:491
  19.4 7.1 %collective-permute-done.4.far = bf16[192,1024]{1,0:T(8,128)(2,1)S(1)} collective-permute-done((bf16[192,1024]{1,0:T(8,128)(2,1)S(1)}, bf16[192,1024]{1,0:T(8,128)(2,1)S(1)}, u32[]{:S(2)}, u32[]{:S(2)}) %collective-permute-start.4) | collective-permute-done | bytes 393248 | tf_op jit(solution)/shard_map/ppermute | solution.py:490
  26.5 1.3 %collective-permute-start.5 = (bf16[192,1024]{1,0:T(8,128)(2,1)S(1)}, bf16[192,1024]{1,0:T(8,128)(2,1)S(1)}, u32[]{:S(2)}, u32[]{:S(2)}) collective-permute-start(bf16[192,1024]{1,0:T(8,128)(2,1)S(1)} %collective-permute-done.4.far), channel_id=1, source_target_pairs={{1,0},{2,3},{5,4},{6,7},{9,8},{10,11},{13,12},{14,15},{17,16},{18,... | collective-permute-start | bytes 1179656 | tf_op jit(solution)/shard_map/ppermute | solution.py:493
  27.8 1.3 %collective-permute-start.1 = (bf16[64,1024]{1,0:T(8,128)(2,1)S(1)}, bf16[64,1024]{1,0:T(8,128)(2,1)S(1)}, u32[]{:S(2)}, u32[]{:S(2)}) collective-permute-start(bf16[64,1024]{1,0:T(8,128)(2,1)S(1)} %get-tuple-element.24.last), channel_id=1, source_target_pairs={{0,1},{3,2},{4,5},{7,6},{8,9},{11,10},{12,13},{15,14},{16,17},{19,... | collective-permute-start | bytes 393224 | tf_op jit(solution)/shard_map/ppermute | solution.py:492
  29.1 2.0 %tables.1 = (s32[64]{0:T(128)S(1)}, s32[64]{0:T(128)S(1)}) custom-call(s32[64]{0:T(128)S(1)} %copy-done.5, s32[64]{0:T(128)S(1)} %copy-done.11), custom_call_target="tpu_custom_call" | custom-call | tf_op jit(solution)/shard_map/tables/pallas_call | solution.py:481
  31.1 3.5 %collective-permute-start.6 = (bf16[64,1024]{1,0:T(8,128)(2,1)S(1)}, bf16[64,1024]{1,0:T(8,128)(2,1)S(1)}, u32[]{:S(2)}, u32[]{:S(2)}) collective-permute-start(bf16[64,1024]{1,0:T(8,128)(2,1)S(1)} %get-tuple-element.29), channel_id=1, source_target_pairs={{1,2},{2,1},{5,6},{6,5},{9,10},{10,9},{13,14},{14,13},{17,18},{18,... | collective-permute-start | bytes 393224 | tf_op jit(solution)/shard_map/ppermute | solution.py:494
  34.6 0.0 collective-permute-done.1.near_last
  34.7 3.5 %collective-permute-start.7 = (bf16[64,1024]{1,0:T(8,128)(2,1)S(1)}, bf16[64,1024]{1,0:T(8,128)(2,1)S(1)}, u32[]{:S(2)}, u32[]{:S(2)}) collective-permute-start(bf16[64,1024]{1,0:T(8,128)(2,1)S(1)} %collective-permute-done.1.near_last), channel_id=1, source_target_pairs={{1,2},{2,1},{5,6},{6,5},{9,10},{10,9},{13,14},{14,13},{17,18},{18,... | collective-permute-start | bytes 393224 | tf_op jit(solution)/shard_map/ppermute | solution.py:495
  38.2 0.0 copy-start
  38.2 1.2 %copy-done = bf16[1024,512]{1,0:T(8,128)(2,1)S(1)} copy-done((bf16[1024,512]{1,0:T(8,128)(2,1)S(1)}, bf16[1024,512]{1,0:T(8,128)(2,1)}, u32[]{:S(2)}) %copy-start) | copy-done | bytes 1048600
  39.4 1.2 %copy-done.2 = bf16[1024,512]{1,0:T(8,128)(2,1)S(1)} copy-done((bf16[1024,512]{1,0:T(8,128)(2,1)S(1)}, bf16[1024,512]{1,0:T(8,128)(2,1)}, u32[]{:S(2)}) %copy-start.2) | copy-done | bytes 1048600
  40.6 3.3 %early.1 = (bf16[704,512]{1,0:T(8,128)(2,1)S(1)}, bf16[704,512]{1,0:T(8,128)(2,1)S(1)}, bf16[288,1024]{1,0:T(8,128)(2,1)S(1)}) custom-call(s32[1]{0:T(128)} %bitcast.me_ref, s32[64]{0:T(128)S(1)} %copy-done.5, s32[64]{0:T(128)S(1)} %get-tuple-element.19.rank_ref, bf16[192,1024]{1,0:T(8,128)(2,1)S(1)} %get-tuple-element.21.low, ...), custom_call_target="tpu_custom_call" | custom-call | flops 1476395008 | bytes 2883584 | tf_op jit(solution)/shard_map/early/pallas_call | solution.py:498
  43.9 0.0 copy-start.1
  43.9 0.6 %middle.1 = (bf16[128,512]{1,0:T(8,128)(2,1)S(1)}, bf16[128,512]{1,0:T(8,128)(2,1)S(1)}) custom-call(s32[1]{0:T(128)} %bitcast.me_ref, bf16[64,1024]{1,0:T(8,128)(2,1)S(1)} %collective-permute-done.6.first, bf16[64,1024]{1,0:T(8,128)(2,1)S(1)} %collective-permute-done.7.second, bf16[1024,512]{1,0:T(8,128)(2,1)S(1)} %copy-done, bf16[1024,512]{1,0:T(8,128)(2,1)S(1)} %copy-done.2), custom_call_target="tpu_custom_call" | custom-call | flops 268435456 | bytes 524288 | tf_op jit(solution)/shard_map/middle/pallas_call | solution.py:511
  44.6 0.5 copy-done.1
  45.1 0.3 copy-done.3
  45.4 9.5 %final.1 = bf16[256,1024]{1,0:T(8,128)(2,1)} custom-call(s32[1]{0:T(128)} %bitcast.me_ref, s32[64]{0:T(128)S(1)} %copy-done.5, s32[64]{0:T(128)S(1)} %copy-done.11, s32[64]{0:T(128)S(1)} %get-tuple-element.19.rank_ref, s32[64]{0:T(128)S(1)} %get-tuple-element.20.key_utt_table, bf16[288,1024]{1,0:T(8,128)(2,1)S(1)} %get-tuple-element.25.early_grouped, ...), custom_call_target="tpu_custom_call" | custom-call | flops 2147483648 | bytes 8388608 | tf_op jit(solution)/shard_map/final/pallas_call | solution.py:520
  (21 shorter events, 0.1 us)
Async XLA Ops:
  0.0 0.7 %copy-start.5 = (s32[64]{0:T(128)S(1)}, s32[64]{0:T(128)}, u32[]{:S(2)}) copy-start(s32[64]{0:T(128)} %source_ref.7) | copy-start | bytes 772
  0.7 1.0 %copy-start.4 = (bf16[256,1024]{1,0:T(8,128)(2,1)S(1)}, bf16[256,1024]{1,0:T(8,128)(2,1)}, u32[]{:S(2)}) copy-start(bf16[256,1024]{1,0:T(8,128)(2,1)} %rows_ref.1) | copy-start | bytes 1572868
  3.7 10.9 %collective-permute-start = (bf16[192,1024]{1,0:T(8,128)(2,1)S(1)}, bf16[192,1024]{1,0:T(8,128)(2,1)S(1)}, u32[]{:S(2)}, u32[]{:S(2)}) collective-permute-start(bf16[192,1024]{1,0:T(8,128)(2,1)S(1)} %get-tuple-element.21.low), channel_id=1, source_target_pairs={{0,1},{1,0},{2,3},{3,2},{4,5},{5,4},{6,7},{7,6},{8,9},{9,8},{10,11... | collective-permute-start | bytes 1179656 | tf_op jit(solution)/shard_map/ppermute | solution.py:479
  3.8 25.3 %copy-start.11 = (s32[64]{0:T(128)S(1)}, s32[64]{0:T(128)}, u32[]{:S(2)}) copy-start(s32[64]{0:T(128)} %utt_ref.3) | copy-start | bytes 772
  3.8 14.3 %collective-permute-start.2 = (bf16[192,1024]{1,0:T(8,128)(2,1)S(1)}, bf16[192,1024]{1,0:T(8,128)(2,1)S(1)}, u32[]{:S(2)}, u32[]{:S(2)}) collective-permute-start(bf16[192,1024]{1,0:T(8,128)(2,1)S(1)} %get-tuple-element.23.high), channel_id=1, source_target_pairs={{1,2},{2,1},{5,6},{6,5},{9,10},{10,9},{13,14},{14,13},{17,18},{18,... | collective-permute-start | bytes 1179656 | tf_op jit(solution)/shard_map/ppermute | solution.py:480
  14.6 11.9 %collective-permute-start.4 = (bf16[192,1024]{1,0:T(8,128)(2,1)S(1)}, bf16[192,1024]{1,0:T(8,128)(2,1)S(1)}, u32[]{:S(2)}, u32[]{:S(2)}) collective-permute-start(bf16[192,1024]{1,0:T(8,128)(2,1)S(1)} %collective-permute-done.near), channel_id=1, source_target_pairs={{1,2},{2,1},{5,6},{6,5},{9,10},{10,9},{13,14},{14,13},{17,18},{18,... | collective-permute-start | bytes 1179656 | tf_op jit(solution)/shard_map/ppermute | solution.py:490
  18.1 20.0 %collective-permute-start.3 = (bf16[192,1024]{1,0:T(8,128)(2,1)S(1)}, bf16[192,1024]{1,0:T(8,128)(2,1)S(1)}, u32[]{:S(2)}, u32[]{:S(2)}) collective-permute-start(bf16[192,1024]{1,0:T(8,128)(2,1)S(1)} %collective-permute-done.2.inner), channel_id=1, source_target_pairs={{1,0},{2,3},{5,4},{6,7},{9,8},{10,11},{13,12},{14,15},{17,16},{18,... | collective-permute-start | bytes 1179656 | tf_op jit(solution)/shard_map/ppermute | solution.py:491
  26.5 18.1 %collective-permute-start.5 = (bf16[192,1024]{1,0:T(8,128)(2,1)S(1)}, bf16[192,1024]{1,0:T(8,128)(2,1)S(1)}, u32[]{:S(2)}, u32[]{:S(2)}) collective-permute-start(bf16[192,1024]{1,0:T(8,128)(2,1)S(1)} %collective-permute-done.4.far), channel_id=1, source_target_pairs={{1,0},{2,3},{5,4},{6,7},{9,8},{10,11},{13,12},{14,15},{17,16},{18,... | collective-permute-start | bytes 1179656 | tf_op jit(solution)/shard_map/ppermute | solution.py:493
  27.8 6.9 %collective-permute-start.1 = (bf16[64,1024]{1,0:T(8,128)(2,1)S(1)}, bf16[64,1024]{1,0:T(8,128)(2,1)S(1)}, u32[]{:S(2)}, u32[]{:S(2)}) collective-permute-start(bf16[64,1024]{1,0:T(8,128)(2,1)S(1)} %get-tuple-element.24.last), channel_id=1, source_target_pairs={{0,1},{3,2},{4,5},{7,6},{8,9},{11,10},{12,13},{15,14},{16,17},{19,... | collective-permute-start | bytes 393224 | tf_op jit(solution)/shard_map/ppermute | solution.py:492
  31.1 12.8 %collective-permute-start.6 = (bf16[64,1024]{1,0:T(8,128)(2,1)S(1)}, bf16[64,1024]{1,0:T(8,128)(2,1)S(1)}, u32[]{:S(2)}, u32[]{:S(2)}) collective-permute-start(bf16[64,1024]{1,0:T(8,128)(2,1)S(1)} %get-tuple-element.29), channel_id=1, source_target_pairs={{1,2},{2,1},{5,6},{6,5},{9,10},{10,9},{13,14},{14,13},{17,18},{18,... | collective-permute-start | bytes 393224 | tf_op jit(solution)/shard_map/ppermute | solution.py:494
  34.7 9.3 %collective-permute-start.7 = (bf16[64,1024]{1,0:T(8,128)(2,1)S(1)}, bf16[64,1024]{1,0:T(8,128)(2,1)S(1)}, u32[]{:S(2)}, u32[]{:S(2)}) collective-permute-start(bf16[64,1024]{1,0:T(8,128)(2,1)S(1)} %collective-permute-done.1.near_last), channel_id=1, source_target_pairs={{1,2},{2,1},{5,6},{6,5},{9,10},{10,9},{13,14},{14,13},{17,18},{18,... | collective-permute-start | bytes 393224 | tf_op jit(solution)/shard_map/ppermute | solution.py:495
  38.2 1.2 %copy-start = (bf16[1024,512]{1,0:T(8,128)(2,1)S(1)}, bf16[1024,512]{1,0:T(8,128)(2,1)}, u32[]{:S(2)}) copy-start(bf16[1024,512]{1,0:T(8,128)(2,1)} %key_weight.5) | copy-start | bytes 3145732
  39.4 1.2 %copy-start.2 = (bf16[1024,512]{1,0:T(8,128)(2,1)S(1)}, bf16[1024,512]{1,0:T(8,128)(2,1)}, u32[]{:S(2)}) copy-start(bf16[1024,512]{1,0:T(8,128)(2,1)} %value_weight.5) | copy-start | bytes 3145732
  40.6 4.0 %copy-start.6 = (bf16[1024,512]{1,0:T(8,128)(2,1)S(1)}, bf16[1024,512]{1,0:T(8,128)(2,1)}, u32[]{:S(2)}) copy-start(bf16[1024,512]{1,0:T(8,128)(2,1)} %query_weight.1) | copy-start | bytes 3145732
  40.6 4.0 %copy-start.7 = (bf16[512,1024]{1,0:T(8,128)(2,1)S(1)}, bf16[512,1024]{1,0:T(8,128)(2,1)}, u32[]{:S(2)}) copy-start(bf16[512,1024]{1,0:T(8,128)(2,1)} %output_weight.1) | copy-start | bytes 3145732
  43.9 1.2 %copy-start.1 = (bf16[1024,512]{1,0:T(8,128)(2,1)S(1)}, bf16[1024,512]{1,0:T(8,128)(2,1)}, u32[]{:S(2)}) copy-start(bf16[1024,512]{1,0:T(8,128)(2,1)} %key_weight.5) | copy-start | bytes 3145732
  43.9 1.5 %copy-start.3 = (bf16[1024,512]{1,0:T(8,128)(2,1)S(1)}, bf16[1024,512]{1,0:T(8,128)(2,1)}, u32[]{:S(2)}) copy-start(bf16[1024,512]{1,0:T(8,128)(2,1)} %value_weight.5) | copy-start | bytes 3145732
  43.9 1.5 %copy-start.8 = (f32[31,1024]{1,0:T(8,128)S(1)}, f32[31,1024]{1,0:T(8,128)}, u32[]{:S(2)}) copy-start(f32[31,1024]{1,0:T(8,128)} %taps.1) | copy-start | bytes 380932
  44.6 0.8 %copy-start.10 = (f32[1024]{0:T(1024)S(1)}, f32[1024]{0:T(1024)}, u32[]{:S(2)}) copy-start(f32[1024]{0:T(1024)} %param.19) | copy-start | bytes 12292
  44.6 0.8 %copy-start.9 = (f32[1024]{0:T(1024)S(1)}, f32[1024]{0:T(1024)}, u32[]{:S(2)}) copy-start(f32[1024]{0:T(1024)} %param.18) | copy-start | bytes 12292

commit v3 on v2

--- a/solution.py
+++ b/solution.py
@@ -8,15 +8,18 @@
 from jax.experimental.pallas import tpu as pltpu
 from jax.sharding import PartitionSpec as P
 
+
 HEADS = 4
 HEAD_DIM = 128
 KERNEL = 31
 TILE = 16
 UTTS = 4
+ARRANGE = 56
 NEGATIVE = -1e30
 
 VMEM = pl.BlockSpec(memory_space=pltpu.VMEM)
 SMEM = pl.BlockSpec(memory_space=pltpu.SMEM)
+HBM = pl.BlockSpec(memory_space=pltpu.HBM)
 
 
 def params(mib):
@@ -250,44 +253,70 @@
     return jnp.where(source_shard % 2 == 1, target, COUNT - 1 - target)
 
 
-def arrange_kernel(me_ref, source_ref, rows_ref, low_ref, last_ref, high_ref, start_ref, filled):
+def divide(value, by):
+    if by & (by - 1) == 0:
+        return value >> (by.bit_length() - 1)
+    return lax.div(value, by)
+
+
+def arrange_kernel(
+    me_ref, source_hbm, rows_hbm, low_ref, last_ref, high_ref, start_ref, source_ref, rows, slots, sems
+):
     me = me_ref[0]
-    tiles_dev = rows_ref.shape[0] // TILE
-    quarter_rows = rows_ref.shape[0] // COUNT
+    rows_dev, quarter_rows = rows.shape[0], last_ref.shape[0]
+    tiles_dev = rows_dev // TILE
+    per_pair = tiles_dev // COUNT
+    rows_copy = pltpu.make_async_copy(rows_hbm, rows, sems.at[0])
+    source_copy = pltpu.make_async_copy(source_hbm, source_ref, sems.at[1])
+    source_copy.start()
+    rows_copy.start()
+    source_copy.wait()
     for target in range(COUNT):
-        filled[target] = 0
-
-    def one(position, carried):
-        source = source_ref[position]
-
-        @pl.when(source // tiles_dev == me)
-        def _():
-            target = position // tiles_dev
-            rank = filled[target]
-            filled[target] = rank + 1
-            quarter = quarter_of(me, target)
-            tile = rows_ref[pl.ds(pl.multiple_of((source % tiles_dev) * TILE, TILE), TILE), :]
-            row = pl.multiple_of(quarter * quarter_rows + rank * TILE, TILE)
-
-            @pl.when(quarter < COUNT - 1)
-            def _():
-                low_ref[pl.ds(row, TILE), :] = tile
-
-            @pl.when(quarter == COUNT - 1)
-            def _():
-                last_ref[pl.ds(pl.multiple_of(rank * TILE, TILE), TILE), :] = tile
-
-            @pl.when(quarter > 0)
-            def _():
-                high_ref[pl.ds(pl.multiple_of(row - quarter_rows, TILE), TILE), :] = tile
-
-            @pl.when(quarter == 0)
-            def _():
-                start_ref[pl.ds(row, TILE), :] = tile
-
-        return carried
-
-    lax.fori_loop(0, COUNT * tiles_dev, one, 0, unroll=4)
+        place = quarter_of(me, target) * per_pair
+        for position in range(target * tiles_dev, (target + 1) * tiles_dev):
+            source = source_ref[position]
+            shard = divide(source, tiles_dev)
+            mine = shard == me
+            slots[jnp.where(mine, place, tiles_dev)] = source - shard * tiles_dev
+            place = place + mine.astype(jnp.int32)
+    rows_copy.wait()
+    for place in range(tiles_dev):
+        tile = rows[pl.ds(pl.multiple_of(slots[place] * TILE, TILE), TILE), :]
+        row = place * TILE
+        if row < rows_dev - quarter_rows:
+            low_ref[row : row + TILE] = tile
+        else:
+            row_here = row - (rows_dev - quarter_rows)
+            last_ref[row_here : row_here + TILE] = tile
+        if row >= quarter_rows:
+            high_ref[row - quarter_rows : row - quarter_rows + TILE] = tile
+        else:
+            start_ref[row : row + TILE] = tile
+
+
+def hold_kernel(*refs):
+    count = (len(refs) - 1) // 2
+    sems = refs[-1]
+    copies = [
+        pltpu.make_async_copy(refs[i], refs[count + i], sems.at[i]) for i in range(count)
+    ]
+    for copy in copies:
+        copy.start()
+    for copy in copies:
+        copy.wait()
+
+
+def hold(*arrays):
+    return pl.pallas_call(
+        hold_kernel,
+        out_shape=tuple(jax.ShapeDtypeStruct(a.shape, a.dtype) for a in arrays),
+        in_specs=[HBM] * len(arrays),
+        out_specs=(VMEM,) * len(arrays),
+        scratch_shapes=[pltpu.SemaphoreType.DMA((len(arrays),))],
+        compiler_params=params(8),
+        cost_estimate=pl.CostEstimate(flops=0, bytes_accessed=8 << 20, transcendentals=0),
+        name="hold_call",
+    )(*arrays)
 
 
 def tables_kernel(source_ref, utt_ref, rank_ref, key_utt_ref, filled):
@@ -468,16 +497,24 @@
 
     low, last, high, start = pl.pallas_call(
         arrange_kernel,
-        out_shape=(shape(piece), shape(quarter), shape(piece), shape(quarter)),
-        in_specs=[SMEM] * 2 + [VMEM],
+        out_shape=tuple(pltpu.VMEM((n, width), frames.dtype) for n in (piece, quarter, piece, quarter)),
+        in_specs=[SMEM] + [HBM] * 2,
         out_specs=(VMEM,) * 4,
-        scratch_shapes=[pltpu.SMEM((COUNT,), jnp.int32)],
-        compiler_params=params(8),
+        scratch_shapes=[
+            pltpu.SMEM((total,), jnp.int32),
+            pltpu.VMEM((rows_dev, width), jnp.bfloat16),
+            pltpu.SMEM((rows_dev // TILE + 1,), jnp.int32),
+            pltpu.SemaphoreType.DMA((2,)),
+        ],
+        compiler_params=params(ARRANGE),
         name="arrange",
     )(me, tile_source, frames)
-    swap = functools.partial(lax.ppermute, axis_name="ctx")
-    near = swap(low, perm=SWAP_OUTER)
-    inner = swap(high, perm=SWAP_INNER)
+
+    def swap(value, perm):
+        return lax.ppermute(value, "ctx", perm)
+
+    near = swap(low, SWAP_OUTER)
+    inner = swap(high, SWAP_INNER)
     rank, key_utt = pl.pallas_call(
         tables_kernel,
         out_shape=(jax.ShapeDtypeStruct((total,), jnp.int32),) * 2,
@@ -485,14 +522,17 @@
         out_specs=(SMEM, SMEM),
         scratch_shapes=[pltpu.SMEM((COUNT * COUNT,), jnp.int32)],
         compiler_params=params(4),
-        name="tables",
+        name="tables_call",
     )(tile_source, tile_utt)
-    far = swap(near, perm=SWAP_INNER)
-    inner_end = swap(inner, perm=TO_ENDS)
-    near_last = swap(after(last, near), perm=FROM_ENDS)
-    far_end = swap(far, perm=TO_ENDS)
-    inner_start = swap(after(start, far), perm=SWAP_INNER)
-    far_last = swap(after(near_last, far), perm=SWAP_INNER)
+    key_weight, value_weight, query_weight, output_weight, depth_weight = hold(
+        key_weight, value_weight, query_weight, output_weight, depth_weight
+    )
+    far = swap(near, SWAP_INNER)
+    inner_end = swap(inner, TO_ENDS)
+    near_last = swap(after(last, near), FROM_ENDS)
+    far_end = swap(far, TO_ENDS)
+    inner_start = swap(after(start, far), SWAP_INNER)
+    far_last = swap(after(near_last, far), SWAP_INNER)
 
     early_rows = rows_dev + 2 * piece + quarter
     early_key, early_value, grouped = pl.pallas_call(
@@ -503,7 +543,7 @@
         scratch_shapes=[pltpu.VMEM((early_rows, width), jnp.bfloat16)],
         compiler_params=params(16),
         cost_estimate=cost(early_rows),
-        name="early",
+        name="early_call",
     )(
         me, tile_source, rank, low, last, high, near, near_last, inner, inner_end,
         key_weight, value_weight,
@@ -515,7 +555,7 @@
         out_specs=(VMEM,) * 2,
         compiler_params=params(8),
         cost_estimate=cost(2 * quarter),
-        name="middle",
+        name="middle_call",
     )(me, inner_start, far_last, key_weight, value_weight)
     return pl.pallas_call(
         final_kernel,

time: 55.3 us -> 55.3 us (level)
  the two profiles are of different devices: /device:TPU:8 before, /device:TPU:10 now
where the time goes in v3:
time: 55.3 us; the launch traced here: 54.9 us
  starting transfers between devices  18.5 us (33%)
  Pallas kernels  16.7 us (30%)
  waiting for transfers between devices  13.9 us (25%)
  local copies, waits for them, and re-layouts  5.59 us (10%)
    ppermute x8, starting transfers between devices, swap(): return lax.ppermute(value, 'ctx', perm)  18.5 us
    ppermute x8, waiting for transfers between devices, swap(): return lax.ppermute(value, 'ctx', perm)  13.9 us
    pallas_call x1, Pallas kernels, line_block(): pl.pallas_call(final_kernel, out_shape=shape(rows_dev), in_specs=[SMEM] *...  9.1 us
    unnamed x18, local copies, waits for them, and re-layouts  5.59 us
    pallas_call x1, Pallas kernels, line_block(): pl.pallas_call(early_kernel, out_shape=(shape(early_rows, wide), shape(ea...  3.26 us
    pallas_call x1, Pallas kernels, line_block(): pl.pallas_call(tables_kernel, out_shape=(jax.ShapeDtypeStruct((total,), j...  2.01 us
    pallas_call x1, Pallas kernels, line_block(): pl.pallas_call(arrange_kernel, out_shape=tuple((pltpu.VMEM((n, width), fr...  1.16 us
  transfers between devices with their start and end apart: 8, of which 3 were waited for; matrix products, arithmetic and copies ran while one was open for 0% of the time, Pallas kernels for 12%

profile of v3, /device:TPU:10, one launch (start us, length us, event | category | flops | bytes accessed | tf_op | source)
XLA Modules:
  0.0 54.9 jit_solution(15328689986543241374)
XLA Ops:
  0.0 1.2 %arrange.1 = (bf16[192,1024]{1,0:T(8,128)(2,1)S(1)}, bf16[64,1024]{1,0:T(8,128)(2,1)S(1)}, bf16[192,1024]{1,0:T(8,128)(2,1)S(1)}, bf16[64,1024]{1,0:T(8,128)(2,1)S(1)}) custom-call(s32[1]{0:T(128)} %bitcast.me_ref, s32[64]{0:T(128)} %source_ref.5, bf16[256,1024]{1,0:T(8,128)(2,1)} %rows_hbm.1), custom_call_target="tpu_custom_call" | custom-call | tf_op jit(solution)/shard_map/arrange/pallas_call | solution.py:498
  1.2 0.5 collective-permute-start
  1.7 4.7 %collective-permute-start.2 = (bf16[192,1024]{1,0:T(8,128)(2,1)S(1)}, bf16[192,1024]{1,0:T(8,128)(2,1)S(1)}, u32[]{:S(2)}, u32[]{:S(2)}) collective-permute-start(bf16[192,1024]{1,0:T(8,128)(2,1)S(1)} %get-tuple-element.28.high), channel_id=1, source_target_pairs={{1,2},{2,1},{5,6},{6,5},{9,10},{10,9},{13,14},{14,13},{17,18},{18,... | collective-permute-start | bytes 1179656 | tf_op jit(solution)/shard_map/ppermute | solution.py:514
  6.4 5.7 %collective-permute-done.near = bf16[192,1024]{1,0:T(8,128)(2,1)S(1)} collective-permute-done((bf16[192,1024]{1,0:T(8,128)(2,1)S(1)}, bf16[192,1024]{1,0:T(8,128)(2,1)S(1)}, u32[]{:S(2)}, u32[]{:S(2)}) %collective-permute-start) | collective-permute-done | bytes 393248 | tf_op jit(solution)/shard_map/ppermute | solution.py:514
  12.1 3.5 %collective-permute-start.4 = (bf16[192,1024]{1,0:T(8,128)(2,1)S(1)}, bf16[192,1024]{1,0:T(8,128)(2,1)S(1)}, u32[]{:S(2)}, u32[]{:S(2)}) collective-permute-start(bf16[192,1024]{1,0:T(8,128)(2,1)S(1)} %collective-permute-done.near), channel_id=1, source_target_pairs={{1,2},{2,1},{5,6},{6,5},{9,10},{10,9},{13,14},{14,13},{17,18},{18,... | collective-permute-start | bytes 1179656 | tf_op jit(solution)/shard_map/ppermute | solution.py:514
  15.6 1.3 %collective-permute-start.3 = (bf16[192,1024]{1,0:T(8,128)(2,1)S(1)}, bf16[192,1024]{1,0:T(8,128)(2,1)S(1)}, u32[]{:S(2)}, u32[]{:S(2)}) collective-permute-start(bf16[192,1024]{1,0:T(8,128)(2,1)S(1)} %collective-permute-done.2.inner), channel_id=1, source_target_pairs={{1,0},{2,3},{5,4},{6,7},{9,8},{10,11},{13,12},{14,15},{17,16},{18,... | collective-permute-start | bytes 1179656 | tf_op jit(solution)/shard_map/ppermute | solution.py:514
  16.9 7.1 %collective-permute-done.4.far = bf16[192,1024]{1,0:T(8,128)(2,1)S(1)} collective-permute-done((bf16[192,1024]{1,0:T(8,128)(2,1)S(1)}, bf16[192,1024]{1,0:T(8,128)(2,1)S(1)}, u32[]{:S(2)}, u32[]{:S(2)}) %collective-permute-start.4) | collective-permute-done | bytes 393248 | tf_op jit(solution)/shard_map/ppermute | solution.py:514
  24.0 1.3 %collective-permute-start.5 = (bf16[192,1024]{1,0:T(8,128)(2,1)S(1)}, bf16[192,1024]{1,0:T(8,128)(2,1)S(1)}, u32[]{:S(2)}, u32[]{:S(2)}) collective-permute-start(bf16[192,1024]{1,0:T(8,128)(2,1)S(1)} %collective-permute-done.4.far), channel_id=1, source_target_pairs={{1,0},{2,3},{5,4},{6,7},{9,8},{10,11},{13,12},{14,15},{17,16},{18,... | collective-permute-start | bytes 1179656 | tf_op jit(solution)/shard_map/ppermute | solution.py:514
  25.3 1.3 %collective-permute-start.1 = (bf16[64,1024]{1,0:T(8,128)(2,1)S(1)}, bf16[64,1024]{1,0:T(8,128)(2,1)S(1)}, u32[]{:S(2)}, u32[]{:S(2)}) collective-permute-start(bf16[64,1024]{1,0:T(8,128)(2,1)S(1)} %get-tuple-element.29.last), channel_id=1, source_target_pairs={{0,1},{3,2},{4,5},{7,6},{8,9},{11,10},{12,13},{15,14},{16,17},{19,... | collective-permute-start | bytes 393224 | tf_op jit(solution)/shard_map/ppermute | solution.py:514
  26.6 2.0 %tables_call.1 = (s32[64]{0:T(128)S(1)}, s32[64]{0:T(128)S(1)}) custom-call(s32[64]{0:T(128)S(1)} %copy-done.5, s32[64]{0:T(128)S(1)} %copy-done.8), custom_call_target="tpu_custom_call" | custom-call | tf_op jit(solution)/shard_map/tables_call/pallas_call | solution.py:518
  28.6 1.2 %copy-done = bf16[1024,512]{1,0:T(8,128)(2,1)S(1)} copy-done((bf16[1024,512]{1,0:T(8,128)(2,1)S(1)}, bf16[1024,512]{1,0:T(8,128)(2,1)}, u32[]{:S(2)}) %copy-start) | copy-done | bytes 1048600
  29.9 1.2 %copy-done.1 = bf16[1024,512]{1,0:T(8,128)(2,1)S(1)} copy-done((bf16[1024,512]{1,0:T(8,128)(2,1)S(1)}, bf16[1024,512]{1,0:T(8,128)(2,1)}, u32[]{:S(2)}) %copy-start.1) | copy-done | bytes 1048600
  31.1 1.2 %copy-done.2 = bf16[1024,512]{1,0:T(8,128)(2,1)S(1)} copy-done((bf16[1024,512]{1,0:T(8,128)(2,1)S(1)}, bf16[1024,512]{1,0:T(8,128)(2,1)}, u32[]{:S(2)}) %copy-start.2) | copy-done | bytes 1048600
  32.3 1.2 %copy-done.3 = bf16[512,1024]{1,0:T(8,128)(2,1)S(1)} copy-done((bf16[512,1024]{1,0:T(8,128)(2,1)S(1)}, bf16[512,1024]{1,0:T(8,128)(2,1)}, u32[]{:S(2)}) %copy-start.3) | copy-done | bytes 1048600
  33.5 0.5 hold_call.1
  34.0 3.5 %collective-permute-start.6 = (bf16[64,1024]{1,0:T(8,128)(2,1)S(1)}, bf16[64,1024]{1,0:T(8,128)(2,1)S(1)}, u32[]{:S(2)}, u32[]{:S(2)}) collective-permute-start(bf16[64,1024]{1,0:T(8,128)(2,1)S(1)} %get-tuple-element.36), channel_id=1, source_target_pairs={{1,2},{2,1},{5,6},{6,5},{9,10},{10,9},{13,14},{14,13},{17,18},{18,... | collective-permute-start | bytes 393224 | tf_op jit(solution)/shard_map/ppermute | solution.py:514
  37.6 2.4 %collective-permute-start.7 = (bf16[64,1024]{1,0:T(8,128)(2,1)S(1)}, bf16[64,1024]{1,0:T(8,128)(2,1)S(1)}, u32[]{:S(2)}, u32[]{:S(2)}) collective-permute-start(bf16[64,1024]{1,0:T(8,128)(2,1)S(1)} %collective-permute-done.1.near_last), channel_id=1, source_target_pairs={{1,2},{2,1},{5,6},{6,5},{9,10},{10,9},{13,14},{14,13},{17,18},{18,... | collective-permute-start | bytes 393224 | tf_op jit(solution)/shard_map/ppermute | solution.py:514
  39.9 3.3 %early_call.1 = (bf16[704,512]{1,0:T(8,128)(2,1)S(1)}, bf16[704,512]{1,0:T(8,128)(2,1)S(1)}, bf16[288,1024]{1,0:T(8,128)(2,1)S(1)}) custom-call(s32[1]{0:T(128)} %bitcast.me_ref, s32[64]{0:T(128)S(1)} %copy-done.5, s32[64]{0:T(128)S(1)} %get-tuple-element.24.rank_ref, bf16[192,1024]{1,0:T(8,128)(2,1)S(1)} %get-tuple-element.26.low, ...), custom_call_target="tpu_custom_call" | custom-call | flops 1476395008 | bytes 2883584 | tf_op jit(solution)/shard_map/early_call/pallas_call | solution.py:538
  43.2 1.2 %collective-permute-done.7.second = bf16[64,1024]{1,0:T(8,128)(2,1)S(1)} collective-permute-done((bf16[64,1024]{1,0:T(8,128)(2,1)S(1)}, bf16[64,1024]{1,0:T(8,128)(2,1)S(1)}, u32[]{:S(2)}, u32[]{:S(2)}) %collective-permute-start.7) | collective-permute-done | bytes 131104 | tf_op jit(solution)/shard_map/ppermute | solution.py:514
  44.4 0.6 %middle_call.1 = (bf16[128,512]{1,0:T(8,128)(2,1)S(1)}, bf16[128,512]{1,0:T(8,128)(2,1)S(1)}) custom-call(s32[1]{0:T(128)} %bitcast.me_ref, bf16[64,1024]{1,0:T(8,128)(2,1)S(1)} %collective-permute-done.6.first, bf16[64,1024]{1,0:T(8,128)(2,1)S(1)} %collective-permute-done.7.second, bf16[1024,512]{1,0:T(8,128)(2,1)S(1)} %get-tuple-element.30.key_weight, ...), custom_call_target="tpu_custom_call" | custom-call | flops 268435456 | bytes 524288 | tf_op jit(solution)/shard_map/middle_call/pallas_call | solution.py:551
  45.1 0.0 copy-start.7
  45.1 0.7 %copy-done.7 = f32[1024]{0:T(1024)S(1)} copy-done((f32[1024]{0:T(1024)S(1)}, f32[1024]{0:T(1024)}, u32[]{:S(2)}) %copy-start.7) | copy-done | bytes 4120
  45.7 0.0 copy-done.6
  45.8 9.1 %final.1 = bf16[256,1024]{1,0:T(8,128)(2,1)} custom-call(s32[1]{0:T(128)} %bitcast.me_ref, s32[64]{0:T(128)S(1)} %copy-done.5, s32[64]{0:T(128)S(1)} %copy-done.8, s32[64]{0:T(128)S(1)} %get-tuple-element.24.rank_ref, s32[64]{0:T(128)S(1)} %get-tuple-element.25.key_utt_table, bf16[288,1024]{1,0:T(8,128)(2,1)S(1)} %get-tuple-element.32.early_grouped, ...), custom_call_target="tpu_custom_call" | custom-call | flops 2147483648 | bytes 8388608 | tf_op jit(solution)/shard_map/final/pallas_call | solution.py:560
  (16 shorter events, 0.0 us)
Async XLA Ops:
  0.0 28.6 %copy-start.4 = (f32[31,1024]{1,0:T(8,128)S(1)}, f32[31,1024]{1,0:T(8,128)}, u32[]{:S(2)}) copy-start(f32[31,1024]{1,0:T(8,128)} %refs_4_.1) | copy-start | bytes 380932
  1.2 10.9 %collective-permute-start = (bf16[192,1024]{1,0:T(8,128)(2,1)S(1)}, bf16[192,1024]{1,0:T(8,128)(2,1)S(1)}, u32[]{:S(2)}, u32[]{:S(2)}) collective-permute-start(bf16[192,1024]{1,0:T(8,128)(2,1)S(1)} %get-tuple-element.26.low), channel_id=1, source_target_pairs={{0,1},{1,0},{2,3},{3,2},{4,5},{5,4},{6,7},{7,6},{8,9},{9,8},{10,11... | collective-permute-start | bytes 1179656 | tf_op jit(solution)/shard_map/ppermute | solution.py:514
  1.7 24.9 %copy-start.5 = (s32[64]{0:T(128)S(1)}, s32[64]{0:T(128)}, u32[]{:S(2)}) copy-start(s32[64]{0:T(128)} %source_ref.5) | copy-start | bytes 772
  1.7 24.9 %copy-start.8 = (s32[64]{0:T(128)S(1)}, s32[64]{0:T(128)}, u32[]{:S(2)}) copy-start(s32[64]{0:T(128)} %utt_ref.3) | copy-start | bytes 772
  1.7 13.9 %collective-permute-start.2 = (bf16[192,1024]{1,0:T(8,128)(2,1)S(1)}, bf16[192,1024]{1,0:T(8,128)(2,1)S(1)}, u32[]{:S(2)}, u32[]{:S(2)}) collective-permute-start(bf16[192,1024]{1,0:T(8,128)(2,1)S(1)} %get-tuple-element.28.high), channel_id=1, source_target_pairs={{1,2},{2,1},{5,6},{6,5},{9,10},{10,9},{13,14},{14,13},{17,18},{18,... | collective-permute-start | bytes 1179656 | tf_op jit(solution)/shard_map/ppermute | solution.py:514
  12.1 11.9 %collective-permute-start.4 = (bf16[192,1024]{1,0:T(8,128)(2,1)S(1)}, bf16[192,1024]{1,0:T(8,128)(2,1)S(1)}, u32[]{:S(2)}, u32[]{:S(2)}) collective-permute-start(bf16[192,1024]{1,0:T(8,128)(2,1)S(1)} %collective-permute-done.near), channel_id=1, source_target_pairs={{1,2},{2,1},{5,6},{6,5},{9,10},{10,9},{13,14},{14,13},{17,18},{18,... | collective-permute-start | bytes 1179656 | tf_op jit(solution)/shard_map/ppermute | solution.py:514
  15.6 24.3 %collective-permute-start.3 = (bf16[192,1024]{1,0:T(8,128)(2,1)S(1)}, bf16[192,1024]{1,0:T(8,128)(2,1)S(1)}, u32[]{:S(2)}, u32[]{:S(2)}) collective-permute-start(bf16[192,1024]{1,0:T(8,128)(2,1)S(1)} %collective-permute-done.2.inner), channel_id=1, source_target_pairs={{1,0},{2,3},{5,4},{6,7},{9,8},{10,11},{13,12},{14,15},{17,16},{18,... | collective-permute-start | bytes 1179656 | tf_op jit(solution)/shard_map/ppermute | solution.py:514
  24.0 21.1 %collective-permute-start.5 = (bf16[192,1024]{1,0:T(8,128)(2,1)S(1)}, bf16[192,1024]{1,0:T(8,128)(2,1)S(1)}, u32[]{:S(2)}, u32[]{:S(2)}) collective-permute-start(bf16[192,1024]{1,0:T(8,128)(2,1)S(1)} %collective-permute-done.4.far), channel_id=1, source_target_pairs={{1,0},{2,3},{5,4},{6,7},{9,8},{10,11},{13,12},{14,15},{17,16},{18,... | collective-permute-start | bytes 1179656 | tf_op jit(solution)/shard_map/ppermute | solution.py:514
  25.3 12.3 %collective-permute-start.1 = (bf16[64,1024]{1,0:T(8,128)(2,1)S(1)}, bf16[64,1024]{1,0:T(8,128)(2,1)S(1)}, u32[]{:S(2)}, u32[]{:S(2)}) collective-permute-start(bf16[64,1024]{1,0:T(8,128)(2,1)S(1)} %get-tuple-element.29.last), channel_id=1, source_target_pairs={{0,1},{3,2},{4,5},{7,6},{8,9},{11,10},{12,13},{15,14},{16,17},{19,... | collective-permute-start | bytes 393224 | tf_op jit(solution)/shard_map/ppermute | solution.py:514
  28.6 1.2 %copy-start = (bf16[1024,512]{1,0:T(8,128)(2,1)S(1)}, bf16[1024,512]{1,0:T(8,128)(2,1)}, u32[]{:S(2)}) copy-start(bf16[1024,512]{1,0:T(8,128)(2,1)} %refs_0_.1) | copy-start | bytes 3145732
  29.9 1.2 %copy-start.1 = (bf16[1024,512]{1,0:T(8,128)(2,1)S(1)}, bf16[1024,512]{1,0:T(8,128)(2,1)}, u32[]{:S(2)}) copy-start(bf16[1024,512]{1,0:T(8,128)(2,1)} %refs_1_.1) | copy-start | bytes 3145732
  31.1 1.2 %copy-start.2 = (bf16[1024,512]{1,0:T(8,128)(2,1)S(1)}, bf16[1024,512]{1,0:T(8,128)(2,1)}, u32[]{:S(2)}) copy-start(bf16[1024,512]{1,0:T(8,128)(2,1)} %refs_2_.1) | copy-start | bytes 3145732
  32.3 1.2 %copy-start.3 = (bf16[512,1024]{1,0:T(8,128)(2,1)S(1)}, bf16[512,1024]{1,0:T(8,128)(2,1)}, u32[]{:S(2)}) copy-start(bf16[512,1024]{1,0:T(8,128)(2,1)} %refs_3_.1) | copy-start | bytes 3145732
  34.0 9.2 %collective-permute-start.6 = (bf16[64,1024]{1,0:T(8,128)(2,1)S(1)}, bf16[64,1024]{1,0:T(8,128)(2,1)S(1)}, u32[]{:S(2)}, u32[]{:S(2)}) collective-permute-start(bf16[64,1024]{1,0:T(8,128)(2,1)S(1)} %get-tuple-element.36), channel_id=1, source_target_pairs={{1,2},{2,1},{5,6},{6,5},{9,10},{10,9},{13,14},{14,13},{17,18},{18,... | collective-permute-start | bytes 393224 | tf_op jit(solution)/shard_map/ppermute | solution.py:514
  37.6 6.9 %collective-permute-start.7 = (bf16[64,1024]{1,0:T(8,128)(2,1)S(1)}, bf16[64,1024]{1,0:T(8,128)(2,1)S(1)}, u32[]{:S(2)}, u32[]{:S(2)}) collective-permute-start(bf16[64,1024]{1,0:T(8,128)(2,1)S(1)} %collective-permute-done.1.near_last), channel_id=1, source_target_pairs={{1,2},{2,1},{5,6},{6,5},{9,10},{10,9},{13,14},{14,13},{17,18},{18,... | collective-permute-start | bytes 393224 | tf_op jit(solution)/shard_map/ppermute | solution.py:514
  45.1 0.7 %copy-start.7 = (f32[1024]{0:T(1024)S(1)}, f32[1024]{0:T(1024)}, u32[]{:S(2)}) copy-start(f32[1024]{0:T(1024)} %param.19) | copy-start | bytes 12292
  45.1 0.7 %copy-start.6 = (f32[1024]{0:T(1024)S(1)}, f32[1024]{0:T(1024)}, u32[]{:S(2)}) copy-start(f32[1024]{0:T(1024)} %param.18) | copy-start | bytes 12292

commit v4 on v3

--- a/solution.py
+++ b/solution.py
@@ -392,11 +392,10 @@
     value_ref[...] = project(normed, value_weight)
 
 
-def middle_kernel(me_ref, first, second, key_weight, value_weight, key_ref, value_ref):
-    rows = jnp.concatenate([first[...], second[...]], axis=0)
-    normed = layer_norm(rows).astype(jnp.bfloat16)
-    key_ref[...] = project(normed, key_weight)
-    value_ref[...] = project(normed, value_weight)
+def lay_kernel(first_ref, second_ref, out_ref):
+    rows = first_ref.shape[0]
+    out_ref[:rows] = first_ref[...]
+    out_ref[rows:] = second_ref[...]
 
 
 def final_kernel(
@@ -524,15 +523,25 @@
         compiler_params=params(4),
         name="tables_call",
     )(tile_source, tile_utt)
-    key_weight, value_weight, query_weight, output_weight, depth_weight = hold(
-        key_weight, value_weight, query_weight, output_weight, depth_weight
+    (
+        key_weight, value_weight, query_weight, output_weight, depth_weight, bn_scale, bn_shift
+    ) = hold(
+        key_weight, value_weight, query_weight, output_weight, depth_weight,
+        bn_scale.reshape(1, -1), bn_shift.reshape(1, -1),
     )
     far = swap(near, SWAP_INNER)
     inner_end = swap(inner, TO_ENDS)
     near_last = swap(after(last, near), FROM_ENDS)
     far_end = swap(far, TO_ENDS)
-    inner_start = swap(after(start, far), SWAP_INNER)
-    far_last = swap(after(near_last, far), SWAP_INNER)
+    rest = pl.pallas_call(
+        lay_kernel,
+        out_shape=shape(2 * quarter),
+        in_specs=[VMEM] * 2,
+        out_specs=VMEM,
+        compiler_params=params(4),
+        name="lay_call",
+    )(start, near_last)
+    rest = swap(after(rest, far), SWAP_INNER)
 
     early_rows = rows_dev + 2 * piece + quarter
     early_key, early_value, grouped = pl.pallas_call(
@@ -549,14 +558,14 @@
         key_weight, value_weight,
     )
     middle_key, middle_value = pl.pallas_call(
-        middle_kernel,
+        key_value_kernel,
         out_shape=(shape(2 * quarter, wide),) * 2,
-        in_specs=[SMEM] + [VMEM] * 4,
+        in_specs=[VMEM] * 3,
         out_specs=(VMEM,) * 2,
         compiler_params=params(8),
         cost_estimate=cost(2 * quarter),
         name="middle_call",
-    )(me, inner_start, far_last, key_weight, value_weight)
+    )(rest, key_weight, value_weight)
     return pl.pallas_call(
         final_kernel,
         out_shape=shape(rows_dev),
@@ -571,8 +580,7 @@
     )(
         me, tile_source, tile_utt, rank, key_utt,
         grouped, far, far_end, early_key, early_value, middle_key, middle_value,
-        key_weight, value_weight, query_weight, output_weight,
-        depth_weight, bn_scale.reshape(1, -1), bn_shift.reshape(1, -1),
+        key_weight, value_weight, query_weight, output_weight, depth_weight, bn_scale, bn_shift,
     )
 
 

time: 55.3 us -> 49.5 us (0.90)
  starting transfers between devices: 18.5 us -> 16 us
  waiting for transfers between devices: 13.9 us -> 11.6 us
  local copies, waits for them, and re-layouts: 5.59 us -> 4.6 us
    ppermute x8 -> x7, starting transfers between devices: 18.5 us -> 16 us  [swap(): return lax.ppermute(value, 'ctx', perm)]
    ppermute x8 -> x7, waiting for transfers between devices: 13.9 us -> 11.6 us  [swap(): return lax.ppermute(value, 'ctx', perm)]
    unnamed x18, local copies, waits for them, and re-layouts: 5.59 us -> 4.6 us
  transfers between devices with their start and end apart: 8 -> 7, of which waited for: 3 -> 2; matrix products, arithmetic and copies ran while one was open for 0% -> 0% of each run, Pallas kernels for 12% -> 13%
where the time goes in v4:
time: 49.5 us; the launch traced here: 49.2 us
  Pallas kernels  16.8 us (34%)
  starting transfers between devices  16 us (32%)
  waiting for transfers between devices  11.6 us (23%)
  local copies, waits for them, and re-layouts  4.6 us (9%)
    ppermute x7, starting transfers between devices, swap(): return lax.ppermute(value, 'ctx', perm)  16 us
    ppermute x7, waiting for transfers between devices, swap(): return lax.ppermute(value, 'ctx', perm)  11.6 us
    pallas_call x1, Pallas kernels, line_block(): pl.pallas_call(final_kernel, out_shape=shape(rows_dev), in_specs=[SMEM] *...  9.13 us
    unnamed x18, local copies, waits for them, and re-layouts  4.6 us
    pallas_call x1, Pallas kernels, line_block(): pl.pallas_call(early_kernel, out_shape=(shape(early_rows, wide), shape(ea...  3.26 us
    pallas_call x1, Pallas kernels, line_block(): pl.pallas_call(tables_kernel, out_shape=(jax.ShapeDtypeStruct((total,), j...  2.01 us
    pallas_call x1, Pallas kernels, line_block(): pl.pallas_call(arrange_kernel, out_shape=tuple((pltpu.VMEM((n, width), fr...  1.22 us
  transfers between devices with their start and end apart: 7, of which 2 were waited for; matrix products, arithmetic and copies ran while one was open for 0% of the time, Pallas kernels for 13%

profile of v4, /device:TPU:10, one launch (start us, length us, event | category | flops | bytes accessed | tf_op | source)
XLA Modules:
  0.0 49.2 jit_solution(15672717634130576255)
XLA Ops:
  0.0 1.2 %arrange.1 = (bf16[192,1024]{1,0:T(8,128)(2,1)S(1)}, bf16[64,1024]{1,0:T(8,128)(2,1)S(1)}, bf16[192,1024]{1,0:T(8,128)(2,1)S(1)}, bf16[64,1024]{1,0:T(8,128)(2,1)S(1)}) custom-call(s32[1]{0:T(128)} %bitcast.me_ref, s32[64]{0:T(128)} %source_ref.5, bf16[256,1024]{1,0:T(8,128)(2,1)} %rows_hbm.1), custom_call_target="tpu_custom_call" | custom-call | tf_op jit(solution)/shard_map/arrange/pallas_call | solution.py:497
  1.2 0.5 %collective-permute-start = (bf16[192,1024]{1,0:T(8,128)(2,1)S(1)}, bf16[192,1024]{1,0:T(8,128)(2,1)S(1)}, u32[]{:S(2)}, u32[]{:S(2)}) collective-permute-start(bf16[192,1024]{1,0:T(8,128)(2,1)S(1)} %get-tuple-element.27.low), channel_id=1, source_target_pairs={{0,1},{1,0},{2,3},{3,2},{4,5},{5,4},{6,7},{7,6},{8,9},{9,8},{10,11... | collective-permute-start | bytes 1179656 | tf_op jit(solution)/shard_map/ppermute | solution.py:513
  1.7 4.6 %collective-permute-start.2 = (bf16[192,1024]{1,0:T(8,128)(2,1)S(1)}, bf16[192,1024]{1,0:T(8,128)(2,1)S(1)}, u32[]{:S(2)}, u32[]{:S(2)}) collective-permute-start(bf16[192,1024]{1,0:T(8,128)(2,1)S(1)} %get-tuple-element.29.high), channel_id=1, source_target_pairs={{1,2},{2,1},{5,6},{6,5},{9,10},{10,9},{13,14},{14,13},{17,18},{18,... | collective-permute-start | bytes 1179656 | tf_op jit(solution)/shard_map/ppermute | solution.py:513
  6.3 5.8 %collective-permute-done.near = bf16[192,1024]{1,0:T(8,128)(2,1)S(1)} collective-permute-done((bf16[192,1024]{1,0:T(8,128)(2,1)S(1)}, bf16[192,1024]{1,0:T(8,128)(2,1)S(1)}, u32[]{:S(2)}, u32[]{:S(2)}) %collective-permute-start) | collective-permute-done | bytes 393248 | tf_op jit(solution)/shard_map/ppermute | solution.py:513
  12.1 3.5 %collective-permute-start.4 = (bf16[192,1024]{1,0:T(8,128)(2,1)S(1)}, bf16[192,1024]{1,0:T(8,128)(2,1)S(1)}, u32[]{:S(2)}, u32[]{:S(2)}) collective-permute-start(bf16[192,1024]{1,0:T(8,128)(2,1)S(1)} %collective-permute-done.near), channel_id=1, source_target_pairs={{1,2},{2,1},{5,6},{6,5},{9,10},{10,9},{13,14},{14,13},{17,18},{18,... | collective-permute-start | bytes 1179656 | tf_op jit(solution)/shard_map/ppermute | solution.py:513
  15.6 1.3 %collective-permute-start.3 = (bf16[192,1024]{1,0:T(8,128)(2,1)S(1)}, bf16[192,1024]{1,0:T(8,128)(2,1)S(1)}, u32[]{:S(2)}, u32[]{:S(2)}) collective-permute-start(bf16[192,1024]{1,0:T(8,128)(2,1)S(1)} %collective-permute-done.2.inner), channel_id=1, source_target_pairs={{1,0},{2,3},{5,4},{6,7},{9,8},{10,11},{13,12},{14,15},{17,16},{18,... | collective-permute-start | bytes 1179656 | tf_op jit(solution)/shard_map/ppermute | solution.py:513
  17.0 1.3 %collective-permute-start.1 = (bf16[64,1024]{1,0:T(8,128)(2,1)S(1)}, bf16[64,1024]{1,0:T(8,128)(2,1)S(1)}, u32[]{:S(2)}, u32[]{:S(2)}) collective-permute-start(bf16[64,1024]{1,0:T(8,128)(2,1)S(1)} %get-tuple-element.30.last), channel_id=1, source_target_pairs={{0,1},{3,2},{4,5},{7,6},{8,9},{11,10},{12,13},{15,14},{16,17},{19,... | collective-permute-start | bytes 393224 | tf_op jit(solution)/shard_map/ppermute | solution.py:513
  18.3 5.8 %collective-permute-done.4.far = bf16[192,1024]{1,0:T(8,128)(2,1)S(1)} collective-permute-done((bf16[192,1024]{1,0:T(8,128)(2,1)S(1)}, bf16[192,1024]{1,0:T(8,128)(2,1)S(1)}, u32[]{:S(2)}, u32[]{:S(2)}) %collective-permute-start.4) | collective-permute-done | bytes 393248 | tf_op jit(solution)/shard_map/ppermute | solution.py:513
  24.0 1.3 %collective-permute-start.5 = (bf16[192,1024]{1,0:T(8,128)(2,1)S(1)}, bf16[192,1024]{1,0:T(8,128)(2,1)S(1)}, u32[]{:S(2)}, u32[]{:S(2)}) collective-permute-start(bf16[192,1024]{1,0:T(8,128)(2,1)S(1)} %collective-permute-done.4.far), channel_id=1, source_target_pairs={{1,0},{2,3},{5,4},{6,7},{9,8},{10,11},{13,12},{14,15},{17,16},{18,... | collective-permute-start | bytes 1179656 | tf_op jit(solution)/shard_map/ppermute | solution.py:513
  25.3 0.0 copy-start.7
  25.4 0.0 copy-start.8
  25.4 0.0 copy-start.6
  25.4 0.0 copy-start.5
  25.4 3.5 %collective-permute-start.6 = (bf16[128,1024]{1,0:T(8,128)(2,1)S(1)}, bf16[128,1024]{1,0:T(8,128)(2,1)S(1)}, u32[]{:S(2)}, u32[]{:S(2)}) collective-permute-start(bf16[128,1024]{1,0:T(8,128)(2,1)S(1)} %lay_call.1), channel_id=1, source_target_pairs={{1,2},{2,1},{5,6},{6,5},{9,10},{10,9},{13,14},{14,13},{17,18},{18,... | collective-permute-start | bytes 786440 | tf_op jit(solution)/shard_map/ppermute | solution.py:513
  28.9 2.0 %tables_call.1 = (s32[64]{0:T(128)S(1)}, s32[64]{0:T(128)S(1)}) custom-call(s32[64]{0:T(128)S(1)} %copy-done.7, s32[64]{0:T(128)S(1)} %copy-done.8), custom_call_target="tpu_custom_call" | custom-call | tf_op jit(solution)/shard_map/tables_call/pallas_call | solution.py:517
  31.0 0.0 copy-start.1
  31.0 1.2 %copy-done.1 = bf16[1024,512]{1,0:T(8,128)(2,1)S(1)} copy-done((bf16[1024,512]{1,0:T(8,128)(2,1)S(1)}, bf16[1024,512]{1,0:T(8,128)(2,1)}, u32[]{:S(2)}) %copy-start.1) | copy-done | bytes 1048600
  32.2 1.2 %copy-done.2 = bf16[1024,512]{1,0:T(8,128)(2,1)S(1)} copy-done((bf16[1024,512]{1,0:T(8,128)(2,1)S(1)}, bf16[1024,512]{1,0:T(8,128)(2,1)}, u32[]{:S(2)}) %copy-start.2) | copy-done | bytes 1048600
  33.4 1.2 %copy-done.3 = bf16[512,1024]{1,0:T(8,128)(2,1)S(1)} copy-done((bf16[512,1024]{1,0:T(8,128)(2,1)S(1)}, bf16[512,1024]{1,0:T(8,128)(2,1)}, u32[]{:S(2)}) %copy-start.3) | copy-done | bytes 1048600
  34.7 0.9 %copy-done.4 = f32[31,1024]{1,0:T(8,128)S(1)} copy-done((f32[31,1024]{1,0:T(8,128)S(1)}, f32[31,1024]{1,0:T(8,128)}, u32[]{:S(2)}) %copy-start.4) | copy-done | bytes 127000
  35.6 0.5 %hold_call.1 = (bf16[1024,512]{1,0:T(8,128)(2,1)S(1)}, bf16[1024,512]{1,0:T(8,128)(2,1)S(1)}, bf16[1024,512]{1,0:T(8,128)(2,1)S(1)}, bf16[512,1024]{1,0:T(8,128)...) custom-call(bf16[1024,512]{1,0:T(8,128)(2,1)S(1)} %copy-done, ...), custom_call_target="tpu_custom_call" | custom-call | bytes 8388608 | tf_op jit(solution)/shard_map/hold_call/pallas_call | solution.py:310
  36.1 3.3 %early_call.1 = (bf16[704,512]{1,0:T(8,128)(2,1)S(1)}, bf16[704,512]{1,0:T(8,128)(2,1)S(1)}, bf16[288,1024]{1,0:T(8,128)(2,1)S(1)}) custom-call(s32[1]{0:T(128)} %bitcast.me_ref, s32[64]{0:T(128)S(1)} %copy-done.7, s32[64]{0:T(128)S(1)} %get-tuple-element.25.rank_ref, bf16[192,1024]{1,0:T(8,128)(2,1)S(1)} %get-tuple-element.27.low, ...), custom_call_target="tpu_custom_call" | custom-call | flops 1476395008 | bytes 2883584 | tf_op jit(solution)/shard_map/early_call/pallas_call | solution.py:547
  39.4 0.6 %middle_call.1 = (bf16[128,512]{1,0:T(8,128)(2,1)S(1)}, bf16[128,512]{1,0:T(8,128)(2,1)S(1)}) custom-call(bf16[128,1024]{1,0:T(8,128)(2,1)S(1)} %collective-permute-done.6.rows_ref, bf16[1024,512]{1,0:T(8,128)(2,1)S(1)} %get-tuple-element.31.key_weight.key_weight_ref, bf16[1024,512]{1,0:T(8,128)(2,1)S(1)} %get-tuple-element.32.value_weight.value_weight_ref), custom_call_target="tpu_custom_call" | custom-call | flops 268435456 | bytes 524288 | tf_op jit(solution)/shard_map/middle_call/pallas_call | solution.py:560
  40.0 9.1 %final.1 = bf16[256,1024]{1,0:T(8,128)(2,1)} custom-call(s32[1]{0:T(128)} %bitcast.me_ref, s32[64]{0:T(128)S(1)} %copy-done.7, s32[64]{0:T(128)S(1)} %copy-done.8, s32[64]{0:T(128)S(1)} %get-tuple-element.25.rank_ref, s32[64]{0:T(128)S(1)} %get-tuple-element.26.key_utt_table, bf16[288,1024]{1,0:T(8,128)(2,1)S(1)} %get-tuple-element.33.early_grouped, ...), custom_call_target="tpu_custom_call" | custom-call | flops 2147483648 | bytes 8388608 | tf_op jit(solution)/shard_map/final/pallas_call | solution.py:569
  (15 shorter events, 0.0 us)
Async XLA Ops:
  0.0 31.0 %copy-start = (bf16[1024,512]{1,0:T(8,128)(2,1)S(1)}, bf16[1024,512]{1,0:T(8,128)(2,1)}, u32[]{:S(2)}) copy-start(bf16[1024,512]{1,0:T(8,128)(2,1)} %refs_0_.1) | copy-start | bytes 3145732
  1.2 10.9 %collective-permute-start = (bf16[192,1024]{1,0:T(8,128)(2,1)S(1)}, bf16[192,1024]{1,0:T(8,128)(2,1)S(1)}, u32[]{:S(2)}, u32[]{:S(2)}) collective-permute-start(bf16[192,1024]{1,0:T(8,128)(2,1)S(1)} %get-tuple-element.27.low), channel_id=1, source_target_pairs={{0,1},{1,0},{2,3},{3,2},{4,5},{5,4},{6,7},{7,6},{8,9},{9,8},{10,11... | collective-permute-start | bytes 1179656 | tf_op jit(solution)/shard_map/ppermute | solution.py:513
  1.7 13.9 %collective-permute-start.2 = (bf16[192,1024]{1,0:T(8,128)(2,1)S(1)}, bf16[192,1024]{1,0:T(8,128)(2,1)S(1)}, u32[]{:S(2)}, u32[]{:S(2)}) collective-permute-start(bf16[192,1024]{1,0:T(8,128)(2,1)S(1)} %get-tuple-element.29.high), channel_id=1, source_target_pairs={{1,2},{2,1},{5,6},{6,5},{9,10},{10,9},{13,14},{14,13},{17,18},{18,... | collective-permute-start | bytes 1179656 | tf_op jit(solution)/shard_map/ppermute | solution.py:513
  12.1 11.9 %collective-permute-start.4 = (bf16[192,1024]{1,0:T(8,128)(2,1)S(1)}, bf16[192,1024]{1,0:T(8,128)(2,1)S(1)}, u32[]{:S(2)}, u32[]{:S(2)}) collective-permute-start(bf16[192,1024]{1,0:T(8,128)(2,1)S(1)} %collective-permute-done.near), channel_id=1, source_target_pairs={{1,2},{2,1},{5,6},{6,5},{9,10},{10,9},{13,14},{14,13},{17,18},{18,... | collective-permute-start | bytes 1179656 | tf_op jit(solution)/shard_map/ppermute | solution.py:513
  15.6 20.5 %collective-permute-start.3 = (bf16[192,1024]{1,0:T(8,128)(2,1)S(1)}, bf16[192,1024]{1,0:T(8,128)(2,1)S(1)}, u32[]{:S(2)}, u32[]{:S(2)}) collective-permute-start(bf16[192,1024]{1,0:T(8,128)(2,1)S(1)} %collective-permute-done.2.inner), channel_id=1, source_target_pairs={{1,0},{2,3},{5,4},{6,7},{9,8},{10,11},{13,12},{14,15},{17,16},{18,... | collective-permute-start | bytes 1179656 | tf_op jit(solution)/shard_map/ppermute | solution.py:513
  17.0 8.4 %collective-permute-start.1 = (bf16[64,1024]{1,0:T(8,128)(2,1)S(1)}, bf16[64,1024]{1,0:T(8,128)(2,1)S(1)}, u32[]{:S(2)}, u32[]{:S(2)}) collective-permute-start(bf16[64,1024]{1,0:T(8,128)(2,1)S(1)} %get-tuple-element.30.last), channel_id=1, source_target_pairs={{0,1},{3,2},{4,5},{7,6},{8,9},{11,10},{12,13},{15,14},{16,17},{19,... | collective-permute-start | bytes 393224 | tf_op jit(solution)/shard_map/ppermute | solution.py:513
  24.0 16.0 %collective-permute-start.5 = (bf16[192,1024]{1,0:T(8,128)(2,1)S(1)}, bf16[192,1024]{1,0:T(8,128)(2,1)S(1)}, u32[]{:S(2)}, u32[]{:S(2)}) collective-permute-start(bf16[192,1024]{1,0:T(8,128)(2,1)S(1)} %collective-permute-done.4.far), channel_id=1, source_target_pairs={{1,0},{2,3},{5,4},{6,7},{9,8},{10,11},{13,12},{14,15},{17,16},{18,... | collective-permute-start | bytes 1179656 | tf_op jit(solution)/shard_map/ppermute | solution.py:513
  25.3 3.6 %copy-start.7 = (s32[64]{0:T(128)S(1)}, s32[64]{0:T(128)}, u32[]{:S(2)}) copy-start(s32[64]{0:T(128)} %source_ref.5) | copy-start | bytes 772
  25.4 3.6 %copy-start.8 = (s32[64]{0:T(128)S(1)}, s32[64]{0:T(128)}, u32[]{:S(2)}) copy-start(s32[64]{0:T(128)} %utt_ref.3) | copy-start | bytes 772
  25.4 5.6 %copy-start.6 = (f32[1024]{0:T(1024)S(1)}, f32[1024]{0:T(1024)}, u32[]{:S(2)}) copy-start(f32[1024]{0:T(1024)} %param.19) | copy-start | bytes 12292
  25.4 5.6 %copy-start.5 = (f32[1024]{0:T(1024)S(1)}, f32[1024]{0:T(1024)}, u32[]{:S(2)}) copy-start(f32[1024]{0:T(1024)} %param.18) | copy-start | bytes 12292
  25.4 14.0 %collective-permute-start.6 = (bf16[128,1024]{1,0:T(8,128)(2,1)S(1)}, bf16[128,1024]{1,0:T(8,128)(2,1)S(1)}, u32[]{:S(2)}, u32[]{:S(2)}) collective-permute-start(bf16[128,1024]{1,0:T(8,128)(2,1)S(1)} %lay_call.1), channel_id=1, source_target_pairs={{1,2},{2,1},{5,6},{6,5},{9,10},{10,9},{13,14},{14,13},{17,18},{18,... | collective-permute-start | bytes 786440 | tf_op jit(solution)/shard_map/ppermute | solution.py:513
  31.0 1.2 %copy-start.1 = (bf16[1024,512]{1,0:T(8,128)(2,1)S(1)}, bf16[1024,512]{1,0:T(8,128)(2,1)}, u32[]{:S(2)}) copy-start(bf16[1024,512]{1,0:T(8,128)(2,1)} %refs_1_.1) | copy-start | bytes 3145732
  32.2 1.2 %copy-start.2 = (bf16[1024,512]{1,0:T(8,128)(2,1)S(1)}, bf16[1024,512]{1,0:T(8,128)(2,1)}, u32[]{:S(2)}) copy-start(bf16[1024,512]{1,0:T(8,128)(2,1)} %refs_2_.1) | copy-start | bytes 3145732
  33.4 1.2 %copy-start.3 = (bf16[512,1024]{1,0:T(8,128)(2,1)S(1)}, bf16[512,1024]{1,0:T(8,128)(2,1)}, u32[]{:S(2)}) copy-start(bf16[512,1024]{1,0:T(8,128)(2,1)} %refs_3_.1) | copy-start | bytes 3145732
  34.7 0.9 %copy-start.4 = (f32[31,1024]{1,0:T(8,128)S(1)}, f32[31,1024]{1,0:T(8,128)}, u32[]{:S(2)}) copy-start(f32[31,1024]{1,0:T(8,128)} %refs_4_.1) | copy-start | bytes 380932
